TPU v7x, 128 devices: a whole 4x4x4 slice. The times are simulated.
128 devices in a mesh: cond: 16 (over z_hi, x, core), ty: 4 (over y), tx: 2 (over z_lo).
Axes of the slice: x: 4, y: 4, z: 4 (z_hi: 2, z_lo: 2; z = z_hi * 2 + z_lo), core: 2. Of those that a mesh axis runs over, the one named last changes fastest.
Arguments:
- bed: float32 [1024, 2048], P('ty', 'tx'), may hold values from -4 to 4
- land_mask: int32 [1024, 2048], P('ty', 'tx'), may hold values 0 or 1
- cell_class: int32 [1024, 2048], P('ty', 'tx'), may hold values from 0 to 2
- weights: int32 [16], replicated, may hold values from 1 to 8
- cond_params: float32 [16, 4], P('cond'), may hold values from 0.25 to 2
- wave_stress: float32 [16, 2, 1024, 2048], P('cond', None, 'ty', 'tx'), may hold values from -0.6 to 0.6
- hydro_state: float32 [16, 3, 1024, 2048], P('cond', None, 'ty', 'tx'), may hold values from -1.8 to 1.8
Outputs:
- bed_next: float32 [1024, 2048], P('ty', 'tx')
- bed_change: float32 [1024, 2048], P('ty', 'tx')
- hydro_next: float32 [16, 3, 1024, 2048], P('cond', None, 'ty', 'tx')
All inputs are finite; a program needn't handle non-finite values. No bound on the sum of `land_mask` on one device may be relied on, other than what follows from the above.
Results may differ from a plain program's by a relative error of at most 0.00002.
Values sent between devices are 32-bit elements; how exact they have to be, the bound alone decides.
A program may use at most 128 MiB of HBM per device.

v0:
```python
import jax
import jax.numpy as jnp
from jax import lax
from jax.sharding import PartitionSpec as P

STEPS = 3


def padded(cells, sides, width):
    for axis, dim in sides:
        count = lax.axis_size(axis)
        ends = count - 1
        head = lax.slice_in_dim(cells, 0, width, axis=dim)
        tail = lax.slice_in_dim(cells, cells.shape[dim] - width, cells.shape[dim], axis=dim)
        cells = jnp.concatenate(
            [
                lax.ppermute(tail, axis, [(i, (i + 1) % count) for i in range(ends)]),
                cells,
                lax.ppermute(head, axis, [((i + 1) % count, i) for i in range(ends)]),
            ],
            axis=dim,
        )
    return cells


def crop(field, width):
    if width == 0:
        return field
    return field[..., width:-width, width:-width]


def advance(level, vel_c, vel_r, depth, relax, inflow, stress_c, stress_r, params):
    tide = params[0] - 1.0
    fric = 0.2 * params[1]
    coef = params[2]
    flow_in = 0.3 * params[3]
    face_c = jnp.sqrt(depth[:, :-1] * depth[:, 1:])
    face_r = jnp.sqrt(depth[:-1, :] * depth[1:, :])
    wet_c = face_c / (face_c + 0.1)
    wet_r = face_r / (face_r + 0.1)
    new_c = (
        (1.0 - fric) * vel_c[:, :-1] - 0.3 * (level[:, 1:] - level[:, :-1]) + stress_c[:, :-1]
    ) * wet_c
    new_r = (
        (1.0 - fric) * vel_r[:-1, :] - 0.3 * (level[1:, :] - level[:-1, :]) + stress_r[:-1, :]
    ) * wet_r
    flux_c = face_c * new_c
    flux_r = face_r * new_r
    inner = level[1:-1, 1:-1]
    new_level = (
        inner
        - (flux_c[1:-1, 1:] - flux_c[1:-1, :-1] + flux_r[1:, 1:-1] - flux_r[:-1, 1:-1])
        + relax[1:-1, 1:-1] * (tide - inner)
        + flow_in * inflow[1:-1, 1:-1]
    )
    load_c = coef * wet_c * new_c * jnp.abs(new_c)
    load_r = coef * wet_r * new_r * jnp.abs(new_r)
    delta = -4.0 * (load_c[1:-1, 1:] - load_c[1:-1, :-1] + load_r[1:, 1:-1] - load_r[:-1, 1:-1])
    return (jnp.stack([new_level, new_c[1:-1, 1:], new_r[1:, 1:-1]]), delta)


def shards(bed, land_mask, cell_class, weights, cond_params, wave_stress, hydro_state):
    ncond = hydro_state.shape[0]
    rows, cols = bed.shape
    reach = STEPS + 1
    wet = land_mask.astype(jnp.float32)
    depth = wet * (1.0 + 0.5 * jnp.tanh(-bed))
    relax = 0.5 * depth * (cell_class == 1).astype(jnp.float32)
    inflow = depth * (cell_class == 2).astype(jnp.float32)
    fixed = jnp.concatenate(
        [jnp.stack([bed, depth, relax, inflow]), wave_stress.reshape(2 * ncond, rows, cols)], axis=0
    )
    fixed_ext = padded(fixed, (("ty", 1), ("tx", 2)), reach)
    extra = 0
    wsum = jnp.sum(weights).astype(jnp.float32)
    first = lax.axis_index("cond") * ncond
    params = cond_params[0]
    change = jnp.zeros((rows + 2 * extra, cols + 2 * extra), jnp.float32)
    state = hydro_state[0]
    local = crop(fixed_ext, reach - 1 - extra)
    for step in range(STEPS):
        widened = padded(state, (("ty", 1), ("tx", 2)), 1 + extra)
        state, delta = advance(
            widened[0],
            widened[1],
            widened[2],
            local[1],
            local[2],
            local[3],
            local[4],
            local[5],
            params,
        )
        change = change + delta
        state = crop(state, extra)
    states = [state]
    share = weights[first + 0].astype(jnp.float32) / wsum
    term = share * change
    merged = lax.psum(term, "cond")
    merged_ext = padded(merged, (("ty", 0), ("tx", 1)), 1)
    height = crop(fixed_ext[0], reach - 1) + merged_ext
    total_cols = cols * lax.axis_size("tx")
    total_rows = rows * lax.axis_size("ty")
    col_ids = lax.axis_index("tx") * cols + jnp.arange(cols + 1, dtype=jnp.int32)[None, :] - 1
    row_ids = lax.axis_index("ty") * rows + jnp.arange(rows + 1, dtype=jnp.int32)[:, None] - 1
    inside_c = ((col_ids >= 0) & (col_ids <= total_cols - 2)).astype(jnp.float32)
    inside_r = ((row_ids >= 0) & (row_ids <= total_rows - 2)).astype(jnp.float32)
    slope_c = (height[:, 1:] - height[:, :-1]) * inside_c
    slope_r = (height[1:, :] - height[:-1, :]) * inside_r
    spill_c = 0.25 * (slope_c - jnp.clip(slope_c, -1.0, 1.0))
    spill_r = 0.25 * (slope_r - jnp.clip(slope_r, -1.0, 1.0))
    bed_next = (
        height[1:-1, 1:-1]
        + spill_c[1:-1, 1:]
        - spill_c[1:-1, :-1]
        + spill_r[1:, 1:-1]
        - spill_r[:-1, 1:-1]
    )
    return (bed_next, crop(merged_ext, 1), jnp.stack(states))


def solution(mesh):
    in_specs = (
        P("ty", "tx"),
        P("ty", "tx"),
        P("ty", "tx"),
        P(),
        P("cond", None),
        P("cond", None, "ty", "tx"),
        P("cond", None, "ty", "tx"),
    )
    out_specs = (P("ty", "tx"), P("ty", "tx"), P("cond", None, "ty", "tx"))
    return jax.shard_map(shards, mesh=mesh, in_specs=in_specs, out_specs=out_specs, check_vma=False)
```

profile of v0, /device:TPU:1, one launch (start us, length us, event | category | flops | bytes accessed | tf_op | source)
XLA Modules:
  0.0 350.1 jit_solution(2181086963215659321)
XLA Ops:
  8.3 4.0 %collective-permute-start.4 = (f32[3,1,1024]{2,1,0:T(1,128)S(1)}, f32[3,1,1024]{2,1,0:T(1,128)S(1)}, u32[]{:S(2)}, u32[]{:S(2)}) collective-permute-start(f32[3,1,1024]{2,1,0:T(1,128)S(1)} %get-tuple-element.44), channel_id=1, source_target_pairs={{0,2},{2,4},{4,6},{1,3},{3,5},{5,7},{8,10},{10,12},{12,14},{9,11},... | collective-permute-start | bytes 36872 | tf_op jit(solution)/shard_map/ppermute | solution.py:17
  19.1 4.2 %collective-permute-start = (f32[6,4,1024]{2,1,0:T(4,128)}, f32[6,4,1024]{2,1,0:T(4,128)S(1)}, u32[]{:S(2)}, u32[]{:S(2)}) collective-permute-start(f32[6,4,1024]{2,1,0:T(4,128)} %get-tuple-element.26), channel_id=1, source_target_pairs={{0,2},{2,4},{4,6},{1,3},{3,5},{5,7},{8,10},{10,12},{12,14},{9,11},... | collective-permute-start | bytes 294920 | tf_op jit(solution)/shard_map/ppermute | solution.py:17
  25.3 4.3 %collective-permute-start.6 = (f32[3,258,1]{2,1,0:T(8,128)S(1)}, f32[3,258,1]{2,1,0:T(8,128)}, u32[]{:S(2)}, u32[]{:S(2)}) collective-permute-start(f32[3,258,1]{2,1,0:T(8,128)S(1)} %get-tuple-element.39), channel_id=1, source_target_pairs={{0,1},{2,3},{4,5},{6,7},{8,9},{10,11},{12,13},{14,15},{16,17},{18,... | collective-permute-start | bytes 9296 | tf_op jit(solution)/shard_map/ppermute | solution.py:17
  33.6 2.5 collective-permute-done.6
  36.1 4.7 %collective-permute-done.7 = f32[3,258,1]{2,1,0:T(8,128)} collective-permute-done((f32[3,258,1]{2,1,0:T(8,128)S(1)}, f32[3,258,1]{2,1,0:T(8,128)}, u32[]{:S(2)}, u32[]{:S(2)}) %collective-permute-start.7) | collective-permute-done | bytes 3128 | tf_op jit(solution)/shard_map/ppermute | solution.py:19
  40.8 4.5 %concatenate.37 = f32[3,258,1026]{2,1,0:T(8,128)} concatenate(f32[3,258,1]{2,1,0:T(8,128)} %collective-permute-done.6, f32[3,258,1024]{2,1,0:T(8,128)S(1)} %pad_maximum_fusion.1, f32[3,258,1]{2,1,0:T(8,128)} %collective-permute-done.7), dimensions={2} | concatenate | bytes 6352992 | tf_op jit(solution)/shard_map/concatenate | solution.py:15
  45.3 3.7 %pad_maximum_fusion = f32[6,264,1024]{2,1,0:T(8,128)S(1)} fusion(f32[6,4,1024]{2,1,0:T(4,128)S(1)} %collective-permute-done.1, f32[6,256,1024]{2,1,0:T(8,128)} %copy-done.26, f32[6,4,1024]{2,1,0:T(4,128)S(1)} %collective-permute-done), kind=kLoop, calls=%fused_computation | loop fusion | flops 3244032 | bytes 12976128 | tf_op jit(solution)/shard_map/concatenate | solution.py:15
  49.0 2.7 copy-done.1
  55.6 3.2 slice_bitcast_fusion.8
  59.4 9.2 %concatenate.35 = f32[6,264,1032]{2,1,0:T(8,128)} concatenate(f32[6,264,4]{2,1,0:T(8,128)S(1)} %copy.22, f32[6,264,1024]{2,1,0:T(8,128)} %copy-done.1, f32[6,264,4]{2,1,0:T(8,128)S(1)} %copy.23), dimensions={2} | concatenate | bytes 13077504 | tf_op jit(solution)/shard_map/concatenate | solution.py:15
  68.7 4.4 %slice_bitcast_fusion.4 = (f32[258,1026]{1,0:T(8,128)S(1)}, f32[258,1026]{1,0:T(8,128)S(1)}, f32[258,1026]{1,0:T(8,128)S(1)}, f32[258,1026]{1,0:T(8,128)S(1)}) fusion(f32[6,264,1032]{2,1,0:T(8,128)} %concatenate.35), kind=kLoop, calls=%fused_computation.46 | loop fusion | bytes 8470656 | tf_op jit(solution)/shard_map/squeeze | solution.py:89
  73.2 6.4 %abs_multiply_fusion.4 = (f32[257,1026]{1,0:T(8,128)}, f32[257,1026]{1,0:T(8,128)S(1)}, f32[257,1026]{1,0:T(8,128)S(1)}) fusion(f32[]{:T(128)} %bitcast.6, f32[6,264,1032]{2,1,0:T(8,128)S(1)} %copy-done, f32[3,258,1026]{2,1,0:T(8,128)} %concatenate.37, f32[]{:T(128)} %bitcast.8), kind=kLoop, calls=%fused_computation.76 | loop fusion | flops 3427866 | bytes 9492560 | tf_op jit(solution)/shard_map/mul | solution.py:57
  79.7 2.8 abs_multiply_fusion.5
  85.5 3.7 %collective-permute-start.8 = (f32[3,1,1024]{2,1,0:T(1,128)S(1)}, f32[3,1,1024]{2,1,0:T(1,128)S(1)}, u32[]{:S(2)}, u32[]{:S(2)}) collective-permute-start(f32[3,1,1024]{2,1,0:T(1,128)S(1)} %get-tuple-element.42), channel_id=1, source_target_pairs={{0,2},{2,4},{4,6},{1,3},{3,5},{5,7},{8,10},{10,12},{12,14},{9,11},... | collective-permute-start | bytes 36872 | tf_op jit(solution)/shard_map/ppermute | solution.py:17
  90.6 3.1 collective-permute-done.9
  96.9 4.0 %collective-permute-start.10 = (f32[3,258,1]{2,1,0:T(8,128)}, f32[3,258,1]{2,1,0:T(8,128)S(1)}, u32[]{:S(2)}, u32[]{:S(2)}) collective-permute-start(f32[3,258,1]{2,1,0:T(8,128)} %get-tuple-element.37), channel_id=1, source_target_pairs={{0,1},{2,3},{4,5},{6,7},{8,9},{10,11},{12,13},{14,15},{16,17},{18,... | collective-permute-start | bytes 9296 | tf_op jit(solution)/shard_map/ppermute | solution.py:17
  102.4 3.6 %collective-permute-done.10 = f32[3,258,1]{2,1,0:T(8,128)S(1)} collective-permute-done((f32[3,258,1]{2,1,0:T(8,128)}, f32[3,258,1]{2,1,0:T(8,128)S(1)}, u32[]{:S(2)}, u32[]{:S(2)}) %collective-permute-start.10) | collective-permute-done | bytes 3128 | tf_op jit(solution)/shard_map/ppermute | solution.py:17
  106.0 3.7 %collective-permute-done.11 = f32[3,258,1]{2,1,0:T(8,128)S(1)} collective-permute-done((f32[3,258,1]{2,1,0:T(8,128)}, f32[3,258,1]{2,1,0:T(8,128)S(1)}, u32[]{:S(2)}, u32[]{:S(2)}) %collective-permute-start.11) | collective-permute-done | bytes 3128 | tf_op jit(solution)/shard_map/ppermute | solution.py:19
  109.7 5.0 %concatenate.39 = f32[3,258,1026]{2,1,0:T(8,128)} concatenate(f32[3,258,1]{2,1,0:T(8,128)S(1)} %collective-permute-done.10, f32[3,258,1024]{2,1,0:T(8,128)} %copy-done.12, f32[3,258,1]{2,1,0:T(8,128)S(1)} %collective-permute-done.11), dimensions={2} | concatenate | bytes 6352992 | tf_op jit(solution)/shard_map/concatenate | solution.py:15
  117.5 3.8 %abs_multiply_fusion.2 = (f32[257,1026]{1,0:T(8,128)}, f32[257,1026]{1,0:T(8,128)S(1)}) fusion(f32[]{:T(128)} %bitcast.6, f32[257,1026]{1,0:T(8,128)S(1)} %get-tuple-element.15, f32[6,264,1032]{2,1,0:T(8,128)} %concatenate.35, f32[3,258,1026]{2,1,0:T(8,128)S(1)} %copy-done.2, f32[]{:T(128)} %bitcast.8), kind=kLoop, calls=%fused_computation.74 | loop fusion | flops 3164184 | bytes 7383104 | tf_op jit(solution)/shard_map/mul | solution.py:57
  128.5 3.2 collective-permute-start.12
  133.0 3.1 collective-permute-done.13
  147.5 3.7 %collective-permute-done.15 = f32[3,258,1]{2,1,0:T(8,128)S(1)} collective-permute-done((f32[3,258,1]{2,1,0:T(8,128)}, f32[3,258,1]{2,1,0:T(8,128)S(1)}, u32[]{:S(2)}, u32[]{:S(2)}) %collective-permute-start.15) | collective-permute-done | bytes 3128 | tf_op jit(solution)/shard_map/ppermute | solution.py:19
  151.3 5.0 %concatenate.41 = f32[3,258,1026]{2,1,0:T(8,128)} concatenate(f32[3,258,1]{2,1,0:T(8,128)S(1)} %collective-permute-done.14, f32[3,258,1024]{2,1,0:T(8,128)} %copy-done.11, f32[3,258,1]{2,1,0:T(8,128)S(1)} %collective-permute-done.15), dimensions={2} | concatenate | bytes 6352992 | tf_op jit(solution)/shard_map/concatenate | solution.py:15
  159.1 3.4 fusion.59
  167.4 3.8 %fusion.39 = f32[256,1024]{1,0:T(8,128)} fusion(f32[257,1026]{1,0:T(8,128)S(1)} %abs_multiply_fusion, f32[258,1025]{1,0:T(8,128)S(1)} %abs_multiply_fusion.1, f32[257,1026]{1,0:T(8,128)S(1)} %copy-done.28, f32[258,1025]{1,0:T(8,128)S(1)} %copy-done.29, f32[257,1026]{1,0:T(8,128)S(1)} %copy-done.30, f32[258,1025]{1,0:T(8,128)S(1)} %copy-done.31, f32[]{:T(128)S(6)} %mul.305), kind=kLoop, calls=%fused_computation.94 | loop fusion | flops 3145728 | bytes 13631492 | tf_op jit(solution)/shard_map/mul | solution.py:98
  171.2 2.6 slice_bitcast_fusion.10
  175.2 3.8 %fusion.37 = f32[1,256,1024]{2,1,0:T(8,128)S(1)} fusion(f32[257,1026]{1,0:T(8,128)S(1)} %copy-done.27, f32[258,1025]{1,0:T(8,128)} %get-tuple-element.6, f32[258,1026]{1,0:T(8,128)S(1)} %copy-done.8, f32[258,1026]{1,0:T(8,128)S(1)} %copy-done.18, f32[258,1026]{1,0:T(8,128)S(1)} %copy-done.15, f32[]{:T(128)} %bitcast.17, f32[]{:T(128)} %bitcast.16), kind=kLoop, calls=%fused_computation.85 | loop fusion | flops 2359296 | bytes 8388616 | tf_op jit(solution)/shard_map/stack | solution.py:59
  179.0 141.5 %all-reduce.2.cloned.1.call-done = f32[256,1024]{1,0:T(8,128)} async-done(((f32[256,1024]{1,0:T(8,128)}), f32[256,1024]{1,0:T(8,128)}) %all-reduce.2.cloned.1.call-update) | async-done | bytes 1048592 | tf_op jit(solution)/shard_map/psum | solution.py:99
  321.4 3.1 collective-permute-start.16
  326.2 2.6 collective-permute-done.17
  339.9 2.4 slice_subtract_fusion.10
  (163 shorter events, 69.8 us)
Async XLA Ops:
  7.2 7.8 %copy-start.10 = (f32[256,1024]{1,0:T(8,128)S(1)}, f32[256,1024]{1,0:T(8,128)}, u32[]{:S(2)}) copy-start(f32[256,1024]{1,0:T(8,128)} %param.7) | copy-start | bytes 3145732
  7.2 7.8 %copy-start.25 = (s32[256,1024]{1,0:T(8,128)S(1)}, s32[256,1024]{1,0:T(8,128)}, u32[]{:S(2)}) copy-start(s32[256,1024]{1,0:T(8,128)} %param.8) | copy-start | bytes 3145732
  7.2 313.3 %all-reduce.2.cloned.1.call-start = ((), (), s32[]{:S(2)}) async-start(), calls=%async_computation | async-start | bytes 2097152 | tf_op jit(solution)/shard_map/psum | solution.py:99
  8.3 16.3 %collective-permute-start.4 = (f32[3,1,1024]{2,1,0:T(1,128)S(1)}, f32[3,1,1024]{2,1,0:T(1,128)S(1)}, u32[]{:S(2)}, u32[]{:S(2)}) collective-permute-start(f32[3,1,1024]{2,1,0:T(1,128)S(1)} %get-tuple-element.44), channel_id=1, source_target_pairs={{0,2},{2,4},{4,6},{1,3},{3,5},{5,7},{8,10},{10,12},{12,14},{9,11},... | collective-permute-start | bytes 36872 | tf_op jit(solution)/shard_map/ppermute | solution.py:17
  12.4 12.3 %collective-permute-start.5 = (f32[3,1,1024]{2,1,0:T(1,128)S(1)}, f32[3,1,1024]{2,1,0:T(1,128)S(1)}, u32[]{:S(2)}, u32[]{:S(2)}) collective-permute-start(f32[3,1,1024]{2,1,0:T(1,128)S(1)} %get-tuple-element.45), channel_id=1, source_target_pairs={{2,0},{4,2},{6,4},{3,1},{5,3},{7,5},{10,8},{12,10},{14,12},{11,9},... | collective-permute-start | bytes 36872 | tf_op jit(solution)/shard_map/ppermute | solution.py:19
  18.2 6.5 %copy-start.38 = (f32[1,3,256,1024]{3,2,1,0:T(8,128)S(1)}, f32[1,3,256,1024]{3,2,1,0:T(8,128)}, u32[]{:S(2)}) copy-start(f32[1,3,256,1024]{3,2,1,0:T(8,128)} %param.13) | copy-start | bytes 9437188
  19.1 26.2 %collective-permute-start = (f32[6,4,1024]{2,1,0:T(4,128)}, f32[6,4,1024]{2,1,0:T(4,128)S(1)}, u32[]{:S(2)}, u32[]{:S(2)}) collective-permute-start(f32[6,4,1024]{2,1,0:T(4,128)} %get-tuple-element.26), channel_id=1, source_target_pairs={{0,2},{2,4},{4,6},{1,3},{3,5},{5,7},{8,10},{10,12},{12,14},{9,11},... | collective-permute-start | bytes 294920 | tf_op jit(solution)/shard_map/ppermute | solution.py:17
  23.3 22.0 %collective-permute-start.1 = (f32[6,4,1024]{2,1,0:T(4,128)S(1)}, f32[6,4,1024]{2,1,0:T(4,128)S(1)}, u32[]{:S(2)}, u32[]{:S(2)}) collective-permute-start(f32[6,4,1024]{2,1,0:T(4,128)S(1)} %get-tuple-element.27), channel_id=1, source_target_pairs={{2,0},{4,2},{6,4},{3,1},{5,3},{7,5},{10,8},{12,10},{14,12},{11,9},... | collective-permute-start | bytes 294920 | tf_op jit(solution)/shard_map/ppermute | solution.py:19
  25.3 10.7 %collective-permute-start.6 = (f32[3,258,1]{2,1,0:T(8,128)S(1)}, f32[3,258,1]{2,1,0:T(8,128)}, u32[]{:S(2)}, u32[]{:S(2)}) collective-permute-start(f32[3,258,1]{2,1,0:T(8,128)S(1)} %get-tuple-element.39), channel_id=1, source_target_pairs={{0,1},{2,3},{4,5},{6,7},{8,9},{10,11},{12,13},{14,15},{16,17},{18,... | collective-permute-start | bytes 9296 | tf_op jit(solution)/shard_map/ppermute | solution.py:17
  29.7 11.1 %collective-permute-start.7 = (f32[3,258,1]{2,1,0:T(8,128)S(1)}, f32[3,258,1]{2,1,0:T(8,128)}, u32[]{:S(2)}, u32[]{:S(2)}) collective-permute-start(f32[3,258,1]{2,1,0:T(8,128)S(1)} %get-tuple-element.38), channel_id=1, source_target_pairs={{1,0},{3,2},{5,4},{7,6},{9,8},{11,10},{13,12},{15,14},{17,16},{19,... | collective-permute-start | bytes 9296 | tf_op jit(solution)/shard_map/ppermute | solution.py:19
  52.4 6.4 %collective-permute-start.2 = (f32[6,264,4]{1,2,0:T(4,128)S(1)}, f32[6,264,4]{1,2,0:T(4,128)S(1)}, u32[]{:S(2)}, u32[]{:S(2)}) collective-permute-start(f32[6,264,4]{1,2,0:T(4,128)S(1)} %copy.20), channel_id=1, source_target_pairs={{0,1},{2,3},{4,5},{6,7},{8,9},{10,11},{12,13},{14,15},{16,17},{18,... | collective-permute-start | bytes 76040 | tf_op jit(solution)/shard_map/ppermute | solution.py:17
  54.1 5.0 %collective-permute-start.3 = (f32[6,264,4]{1,2,0:T(4,128)S(1)}, f32[6,264,4]{1,2,0:T(4,128)S(1)}, u32[]{:S(2)}, u32[]{:S(2)}) collective-permute-start(f32[6,264,4]{1,2,0:T(4,128)S(1)} %copy.21), channel_id=1, source_target_pairs={{1,0},{3,2},{5,4},{7,6},{9,8},{11,10},{13,12},{15,14},{17,16},{19,... | collective-permute-start | bytes 76040 | tf_op jit(solution)/shard_map/ppermute | solution.py:19
  73.1 6.6 %copy-start.4 = (f32[258,1026]{1,0:T(8,128)}, f32[258,1026]{1,0:T(8,128)S(1)}, u32[]{:S(2)}) copy-start(f32[258,1026]{1,0:T(8,128)S(1)} %get-tuple-element.22) | copy-start | bytes 3176500
  73.1 10.3 %copy-start.13 = (f32[258,1026]{1,0:T(8,128)}, f32[258,1026]{1,0:T(8,128)S(1)}, u32[]{:S(2)}) copy-start(f32[258,1026]{1,0:T(8,128)S(1)} %get-tuple-element.20) | copy-start | bytes 3176500
  73.1 10.3 %copy-start.16 = (f32[258,1026]{1,0:T(8,128)}, f32[258,1026]{1,0:T(8,128)S(1)}, u32[]{:S(2)}) copy-start(f32[258,1026]{1,0:T(8,128)S(1)} %get-tuple-element.21) | copy-start | bytes 3176500
  73.2 6.5 %copy-start.9 = (f32[258,1026]{1,0:T(8,128)S(1)}, f32[258,1026]{1,0:T(8,128)}, u32[]{:S(2)}) copy-start(f32[258,1026]{1,0:T(8,128)} %get-tuple-element.33) | copy-start | bytes 3176500
  73.2 6.5 %copy-start.33 = (f32[258,1026]{1,0:T(8,128)S(1)}, f32[258,1026]{1,0:T(8,128)}, u32[]{:S(2)}) copy-start(f32[258,1026]{1,0:T(8,128)} %get-tuple-element.32) | copy-start | bytes 3176500
  85.5 5.0 %collective-permute-start.8 = (f32[3,1,1024]{2,1,0:T(1,128)S(1)}, f32[3,1,1024]{2,1,0:T(1,128)S(1)}, u32[]{:S(2)}, u32[]{:S(2)}) collective-permute-start(f32[3,1,1024]{2,1,0:T(1,128)S(1)} %get-tuple-element.42), channel_id=1, source_target_pairs={{0,2},{2,4},{4,6},{1,3},{3,5},{5,7},{8,10},{10,12},{12,14},{9,11},... | collective-permute-start | bytes 36872 | tf_op jit(solution)/shard_map/ppermute | solution.py:17
  89.3 4.4 %collective-permute-start.9 = (f32[3,1,1024]{2,1,0:T(1,128)S(1)}, f32[3,1,1024]{2,1,0:T(1,128)S(1)}, u32[]{:S(2)}, u32[]{:S(2)}) collective-permute-start(f32[3,1,1024]{2,1,0:T(1,128)S(1)} %get-tuple-element.43), channel_id=1, source_target_pairs={{2,0},{4,2},{6,4},{3,1},{5,3},{7,5},{10,8},{12,10},{14,12},{11,9},... | collective-permute-start | bytes 36872 | tf_op jit(solution)/shard_map/ppermute | solution.py:19
  96.9 9.1 %collective-permute-start.10 = (f32[3,258,1]{2,1,0:T(8,128)}, f32[3,258,1]{2,1,0:T(8,128)S(1)}, u32[]{:S(2)}, u32[]{:S(2)}) collective-permute-start(f32[3,258,1]{2,1,0:T(8,128)} %get-tuple-element.37), channel_id=1, source_target_pairs={{0,1},{2,3},{4,5},{6,7},{8,9},{10,11},{12,13},{14,15},{16,17},{18,... | collective-permute-start | bytes 9296 | tf_op jit(solution)/shard_map/ppermute | solution.py:17
  100.9 8.9 %collective-permute-start.11 = (f32[3,258,1]{2,1,0:T(8,128)}, f32[3,258,1]{2,1,0:T(8,128)S(1)}, u32[]{:S(2)}, u32[]{:S(2)}) collective-permute-start(f32[3,258,1]{2,1,0:T(8,128)} %get-tuple-element.36), channel_id=1, source_target_pairs={{1,0},{3,2},{5,4},{7,6},{9,8},{11,10},{13,12},{15,14},{17,16},{19,... | collective-permute-start | bytes 9296 | tf_op jit(solution)/shard_map/ppermute | solution.py:19
  128.5 4.5 %collective-permute-start.12 = (f32[3,1,1024]{2,1,0:T(1,128)S(1)}, f32[3,1,1024]{2,1,0:T(1,128)S(1)}, u32[]{:S(2)}, u32[]{:S(2)}) collective-permute-start(f32[3,1,1024]{2,1,0:T(1,128)S(1)} %get-tuple-element.40), channel_id=1, source_target_pairs={{0,2},{2,4},{4,6},{1,3},{3,5},{5,7},{8,10},{10,12},{12,14},{9,11},... | collective-permute-start | bytes 36872 | tf_op jit(solution)/shard_map/ppermute | solution.py:17
  131.7 4.4 %collective-permute-start.13 = (f32[3,1,1024]{2,1,0:T(1,128)S(1)}, f32[3,1,1024]{2,1,0:T(1,128)S(1)}, u32[]{:S(2)}, u32[]{:S(2)}) collective-permute-start(f32[3,1,1024]{2,1,0:T(1,128)S(1)} %get-tuple-element.41), channel_id=1, source_target_pairs={{2,0},{4,2},{6,4},{3,1},{5,3},{7,5},{10,8},{12,10},{14,12},{11,9},... | collective-permute-start | bytes 36872 | tf_op jit(solution)/shard_map/ppermute | solution.py:19
  140.8 6.7 %collective-permute-start.14 = (f32[3,258,1]{2,1,0:T(8,128)}, f32[3,258,1]{2,1,0:T(8,128)S(1)}, u32[]{:S(2)}, u32[]{:S(2)}) collective-permute-start(f32[3,258,1]{2,1,0:T(8,128)} %get-tuple-element.35), channel_id=1, source_target_pairs={{0,1},{2,3},{4,5},{6,7},{8,9},{10,11},{12,13},{14,15},{16,17},{18,... | collective-permute-start | bytes 9296 | tf_op jit(solution)/shard_map/ppermute | solution.py:17
  142.4 8.9 %collective-permute-start.15 = (f32[3,258,1]{2,1,0:T(8,128)}, f32[3,258,1]{2,1,0:T(8,128)S(1)}, u32[]{:S(2)}, u32[]{:S(2)}) collective-permute-start(f32[3,258,1]{2,1,0:T(8,128)} %get-tuple-element.34), channel_id=1, source_target_pairs={{1,0},{3,2},{5,4},{7,6},{9,8},{11,10},{13,12},{15,14},{17,16},{19,... | collective-permute-start | bytes 9296 | tf_op jit(solution)/shard_map/ppermute | solution.py:19
  167.4 7.8 %copy-start.27 = (f32[257,1026]{1,0:T(8,128)S(1)}, f32[257,1026]{1,0:T(8,128)}, u32[]{:S(2)}) copy-start(f32[257,1026]{1,0:T(8,128)} %get-tuple-element.8) | copy-start | bytes 3164188
  175.2 150.6 %copy-start.20 = (f32[257,1026]{1,0:T(8,128)S(1)}, f32[257,1026]{1,0:T(8,128)}, u32[]{:S(2)}) copy-start(f32[257,1026]{1,0:T(8,128)} %copy-done.19) | copy-start | bytes 3164188
  320.5 8.3 %copy-start.34 = (f32[256,1024]{1,0:T(8,128)S(1)}, f32[256,1024]{1,0:T(8,128)}, u32[]{:S(2)}) copy-start(f32[256,1024]{1,0:T(8,128)} %all-reduce.2.cloned.1.call-done) | copy-start | bytes 3145732
  321.4 4.9 %collective-permute-start.16 = (f32[1,1024]{1,0:T(1,128)S(1)}, f32[1,1024]{1,0:T(1,128)S(1)}, u32[]{:S(2)}, u32[]{:S(2)}) collective-permute-start(f32[1,1024]{1,0:T(1,128)S(1)} %get-tuple-element.48), channel_id=1, source_target_pairs={{0,2},{2,4},{4,6},{1,3},{3,5},{5,7},{8,10},{10,12},{12,14},{9,11},... | collective-permute-start | bytes 12296 | tf_op jit(solution)/shard_map/ppermute | solution.py:17
  324.5 4.4 %collective-permute-start.17 = (f32[1,1024]{1,0:T(1,128)S(1)}, f32[1,1024]{1,0:T(1,128)S(1)}, u32[]{:S(2)}, u32[]{:S(2)}) collective-permute-start(f32[1,1024]{1,0:T(1,128)S(1)} %get-tuple-element.49), channel_id=1, source_target_pairs={{2,0},{4,2},{6,4},{3,1},{5,3},{7,5},{10,8},{12,10},{14,12},{11,9},... | collective-permute-start | bytes 12296 | tf_op jit(solution)/shard_map/ppermute | solution.py:19
  329.0 5.5 %collective-permute-start.18 = (f32[258,1]{1,0:T(8,128)S(1)}, f32[258,1]{1,0:T(8,128)S(1)}, u32[]{:S(2)}, u32[]{:S(2)}) collective-permute-start(f32[258,1]{1,0:T(8,128)S(1)} %get-tuple-element.47), channel_id=1, source_target_pairs={{0,1},{2,3},{4,5},{6,7},{8,9},{10,11},{12,13},{14,15},{16,17},{18,... | collective-permute-start | bytes 3104 | tf_op jit(solution)/shard_map/ppermute | solution.py:17
  331.3 5.9 %collective-permute-start.19 = (f32[258,1]{1,0:T(8,128)S(1)}, f32[258,1]{1,0:T(8,128)}, u32[]{:S(2)}, u32[]{:S(2)}) collective-permute-start(f32[258,1]{1,0:T(8,128)S(1)} %get-tuple-element.46), channel_id=1, source_target_pairs={{1,0},{3,2},{5,4},{7,6},{9,8},{11,10},{13,12},{15,14},{17,16},{19,... | collective-permute-start | bytes 3104 | tf_op jit(solution)/shard_map/ppermute | solution.py:19
  (32 other events, 92.7 us)
Sparse Core Ops, SparseCore 0:
  171.3 149.1 all-reduce.1
where the time goes:
time: 354 us; the launch traced here: 350 us
  waiting for transfers between devices  171 us (48%)
  local copies, waits for them, and re-layouts  66.4 us (19%)
  other arithmetic  48.9 us (14%)
  starting transfers between devices  45.4 us (13%)
  between operations  18.2 us (5%)
    psum x1, waiting for transfers between devices, shards(): merged = lax.psum(term, 'cond')  141 us
    ppermute x10, starting transfers between devices, padded(): lax.ppermute(tail, axis, [(i, (i + 1) % count) for i in range(ends)])  31.7 us
    concatenate x5, local copies, waits for them, and re-layouts, padded(): jnp.concatenate([lax.ppermute(tail, axis, [(i, (i + 1) % count) for i in...  25.4 us
    ppermute x10, waiting for transfers between devices, padded(): lax.ppermute(head, axis, [((i + 1) % count, i) for i in range(ends)])  23 us
    unnamed x88, local copies, waits for them, and re-layouts  15.5 us
    ppermute x10, starting transfers between devices, padded(): lax.ppermute(head, axis, [((i + 1) % count, i) for i in range(ends)])  13.6 us
    mul x3, other arithmetic, advance(): load_r = coef * wet_r * new_r * jnp.abs(new_r)  11.4 us
    another operation x3, other arithmetic, advance(): return (jnp.stack([new_level, new_c[1:-1, 1:], new_r[1:, 1:-1]]), delta)  8.04 us
  transfers between devices with their start and end apart: 21, of which 11 were waited for; matrix products, arithmetic and copies ran while one was open for 7% of the time, Pallas kernels for 0%

commit v1 on v0

v1 whole, which is shorter than its diff:
```python
import functools

import jax
import jax.numpy as jnp
from jax import lax
from jax.experimental import pallas as pl
from jax.experimental.pallas import tpu as pltpu
from jax.sharding import PartitionSpec as P

MESH = pl.DeviceIdType.MESH
F32 = jnp.float32
LANE = 128
EDGE = 8
HALO = 4
R = 16
NX = 4
CHUNKS = (5, 4, 4, 4)


def kernel(
    rows,
    cols,
    chunks,
    bed_h,
    mask_h,
    cls_h,
    wts,
    par,
    stress_h,
    hydro_h,
    bn_h,
    bc_h,
    hy_h,
    E,
    U,
    V,
    SX,
    SY,
    BED,
    MASK,
    CLS,
    D,
    WC,
    WR,
    FC,
    FR,
    A,
    B,
    QC,
    QR,
    T,
    M,
    BN,
    CF,
    CQ,
    EDF,
    EDI,
    PS,
    RSTRIP,
    CR,
    PP,
    RAL,
    RAR,
    RBL,
    RBR,
    RCL,
    RCR,
    C1,
    C2,
    S,
    RZ,
    in_sem,
    edge_sem,
    halo_send,
    halo_recv,
    strip_send,
    strip_recv,
    ring_send,
    ring_recv,
    out_sem,
):
    nrow = rows + 2 * EDGE
    width = cols + LANE
    nblk = nrow // R
    c = lax.axis_index("cond")
    ty = lax.axis_index("ty")
    tx = lax.axis_index("tx")
    nty = lax.axis_size("ty")
    ntx = lax.axis_size("tx")
    core = c % 2
    x = (c // 2) % NX
    zh = c // (2 * NX)
    up = (ty + nty - 1) % nty
    down = (ty + 1) % nty
    side = 1 - tx
    xr = (x + 1) % NX
    xl = (x + NX - 1) % NX
    xf = (x + 2) % NX

    def cond_of(z, xx, k):
        return (z * NX + xx) * 2 + k

    sibling = (cond_of(zh, x, 1 - core), ty, tx)
    right = (cond_of(zh, xr, core), ty, tx)
    left = (cond_of(zh, xl, core), ty, tx)
    zpeer = (cond_of(1 - zh, x, core), ty, tx)
    above = (c, up, tx)
    below = (c, down, tx)
    beside = (c, ty, side)
    diag_up = (c, up, side)
    diag_down = (c, down, side)

    fields = (E, U, V, SX, SY, BED, MASK, CLS)
    sources = (
        hydro_h.at[0, 0],
        hydro_h.at[0, 1],
        hydro_h.at[0, 2],
        stress_h.at[0, 0],
        stress_h.at[0, 1],
        bed_h,
        mask_h,
        cls_h,
    )
    edge_at = pl.multiple_of((1 - tx) * (cols - LANE), LANE)
    edges = [EDF.at[i] for i in range(6)] + [EDI.at[i] for i in range(2)]

    edge_copies = [
        pltpu.make_async_copy(src.at[:, pl.ds(edge_at, LANE)], dst, edge_sem.at[i])
        for i, (src, dst) in enumerate(zip(sources, edges))
    ]
    for copy in edge_copies:
        copy.start()
    in_copies = [
        pltpu.make_async_copy(src, dst.at[EDGE : EDGE + rows, 0:cols], in_sem.at[i])
        for i, (src, dst) in enumerate(zip(sources, fields))
    ]
    for i in (5, 6, 0, 1, 2, 3, 4, 7):
        in_copies[i].start()

    pad = EDGE - HALO
    for field in fields:
        field[0:pad, 0:cols] = jnp.zeros((pad, cols), field.dtype)
        field[nrow - pad : nrow, 0:cols] = jnp.zeros((pad, cols), field.dtype)
    E[nrow : nrow + 8, :] = jnp.zeros((8, width), F32)
    D[nrow : nrow + 8, :] = jnp.zeros((8, width), F32)
    M[0:EDGE, cols:width] = jnp.zeros((EDGE, LANE), F32)
    M[nrow - EDGE : nrow, cols:width] = jnp.zeros((EDGE, LANE), F32)

    barrier = pltpu.get_barrier_semaphore()
    peers = (sibling, right, left, zpeer, above, below, beside, diag_up, diag_down)
    for peer in peers:
        pl.semaphore_signal(barrier, inc=1, device_id=peer, device_id_type=MESH)
    pl.semaphore_wait(barrier, len(peers))

    def remote(src, dst, send, recv, peer):
        copy = pltpu.make_async_remote_copy(
            src_ref=src, dst_ref=dst, send_sem=send, recv_sem=recv, device_id=peer, device_id_type=MESH
        )
        copy.start()
        return copy

    halo_copies = []
    for i, (src, dst) in enumerate(zip(sources, fields)):
        halo_copies.append(
            remote(
                src.at[rows - HALO : rows, :],
                dst.at[EDGE - HALO : EDGE, 0:cols],
                halo_send.at[0, i],
                halo_recv.at[0, i],
                below,
            )
        )
        halo_copies.append(
            remote(
                src.at[0:HALO, :],
                dst.at[EDGE + rows : EDGE + rows + HALO, 0:cols],
                halo_send.at[1, i],
                halo_recv.at[1, i],
                above,
            )
        )

    lanes = lax.broadcasted_iota(jnp.int32, (R, LANE), 1)
    for copy in edge_copies:
        copy.wait()

    def pack(i, carry):
        r = pl.multiple_of(i * R, R)
        strip = jnp.zeros((R, LANE), F32)
        for k in range(8):
            cells = edges[k][pl.ds(r, R), :].astype(F32)
            cells = pltpu.roll(cells, HALO * k + HALO * (1 - tx), 1)
            strip = jnp.where((lanes >= HALO * k) & (lanes < HALO * (k + 1)), cells, strip)
        PS[pl.ds(r, R), :] = strip
        return carry

    lax.fori_loop(0, rows // R, pack, 0)
    strip_copies = [
        remote(PS, RSTRIP.at[EDGE : EDGE + rows], strip_send.at[0], strip_recv.at[0], beside),
        remote(PS.at[rows - 8 : rows], RSTRIP.at[0:8], strip_send.at[1], strip_recv.at[1], diag_down),
        remote(PS.at[0:8], RSTRIP.at[nrow - 8 : nrow], strip_send.at[2], strip_recv.at[2], diag_up),
    ]

    def depth_of(mask, bed):
        return mask.astype(F32) * (1.0 + 0.5 * jnp.tanh(-bed))

    in_copies[5].wait()
    in_copies[6].wait()

    def depth_inner(i, carry):
        r = pl.multiple_of(i * R, R)
        D[pl.ds(r, R), 0:cols] = depth_of(MASK[pl.ds(r, R), 0:cols], BED[pl.ds(r, R), 0:cols])
        return carry

    lax.fori_loop(1, nblk - 1, depth_inner, 0)
    for copy in halo_copies:
        copy.wait_recv()
    for copy in strip_copies:
        copy.wait_recv()

    row_ids = lax.broadcasted_iota(jnp.int32, (R, LANE), 0)

    def unpack(i, carry):
        r = pl.multiple_of(i * R, R)
        strip = RSTRIP[pl.ds(r, R), :]
        inner = (lanes < HALO) & (tx == 0) | (lanes >= LANE - HALO) & (tx == 1)
        for k in range(8):
            shift = (LANE - HALO * k) * (1 - tx) + (LANE - HALO - HALO * k) * tx
            cells = jnp.where(inner, pltpu.roll(strip, shift % LANE, 1), 0.0)
            fields[k][pl.ds(r, R), cols:width] = cells.astype(fields[k].dtype)
        depth = depth_of(MASK[pl.ds(r, R), cols:width], BED[pl.ds(r, R), cols:width])
        at = row_ids + r
        real = ((at >= EDGE) | (ty > 0)) & ((at < EDGE + rows) | (ty < nty - 1))
        D[pl.ds(r, R), cols:width] = jnp.where(real, depth, 0.0)
        return carry

    lax.fori_loop(0, nblk, unpack, 0)
    wide_rows = lax.broadcasted_iota(jnp.int32, (R, cols), 0)
    for r in (0, nrow - R):
        depth = depth_of(MASK[r : r + R, 0:cols], BED[r : r + R, 0:cols])
        at = wide_rows + r
        real = ((at >= EDGE) | (ty > 0)) & ((at < EDGE + rows) | (ty < nty - 1))
        D[r : r + R, 0:cols] = jnp.where(real, depth, 0.0)

    for i in (0, 1, 2, 3, 4, 7):
        in_copies[i].wait()

    tide = par[0, 0] - 1.0
    fric = 0.2 * par[0, 1]
    coef = par[0, 2]
    flow_in = 0.3 * par[0, 3]
    keep = 1.0 - fric
    total = wts[0]
    for i in range(1, 16):
        total = total + wts[i]
    one = jnp.ones((1, width), F32)
    scale = one * (-4.0 * coef * wts[c].astype(F32)) / (one * total.astype(F32))

    def south(y):
        return pltpu.roll(y, R + 7, 0)[:R]

    def north(before, y):
        return pltpu.roll(jnp.concatenate([before, y], axis=0), 1, 0)[8:]

    def east(y):
        return pltpu.roll(y, width - 1, 1)

    def west(y):
        return pltpu.roll(y, 1, 1)

    def advance(step, i, carry):
        r = pl.multiple_of(i * R, R)
        here = pl.ds(r, R)
        level = E[pl.ds(r, R + 8), :]
        if step == 0:
            level = 0.3 * level
            deep = D[pl.ds(r, R + 8), :]
            depth = deep[:R]
            face_c = jnp.sqrt(depth * east(depth))
            face_r = jnp.sqrt(depth * south(deep))
            wet_c = face_c / (face_c + 0.1)
            wet_r = face_r / (face_r + 0.1)
            face_c = 0.3 * face_c
            face_r = 0.3 * face_r
            kind = CLS[here, :]
            relax = jnp.where(kind == 1, 0.5 * depth, 0.0)
            add = 0.3 * (relax * tide + flow_in * jnp.where(kind == 2, depth, 0.0))
            stay = 1.0 - relax
            WC[here, :] = wet_c
            WR[here, :] = wet_r
            FC[here, :] = face_c
            FR[here, :] = face_r
            A[here, :] = add
            B[here, :] = stay
        else:
            wet_c = WC[here, :]
            wet_r = WR[here, :]
            face_c = FC[here, :]
            face_r = FR[here, :]
            add = A[here, :]
            stay = B[here, :]
        mid = level[:R]
        vel_c = (keep * U[here, :] - (east(mid) - mid) + SX[here, :]) * wet_c
        vel_r = (keep * V[here, :] - (south(level) - mid) + SY[here, :]) * wet_r
        U[here, :] = vel_c
        V[here, :] = vel_r
        flux_c = face_c * vel_c
        flux_r = face_r * vel_r
        level = mid * stay + add - (flux_c - west(flux_c)) - (flux_r - north(carry[0], flux_r))
        if step == 2:
            level = level * (1.0 / 0.3)
        E[here, :] = level
        load_c = wet_c * vel_c * jnp.abs(vel_c)
        load_r = wet_r * vel_r * jnp.abs(vel_r)
        if step > 0:
            load_c = load_c + QC[here, :]
            load_r = load_r + QR[here, :]
        if step < 2:
            QC[here, :] = load_c
            QR[here, :] = load_r
            return (flux_r[R - 8 :],)
        T[here, :] = scale * (load_c - west(load_c) + load_r - north(carry[1], load_r))
        return (flux_r[R - 8 :], load_r[R - 8 :])

    done = [0, 0, 0]

    def run(step, stop):
        stop = min(stop, nblk)
        start = done[step]
        if stop <= start:
            return
        done[step] = stop
        if start == 0:
            carry = (jnp.zeros((8, width), F32),) * (2 if step == 2 else 1)
        else:
            carry = (CF[step],) + ((CQ[...],) if step == 2 else ())
        carry = lax.fori_loop(start, stop, functools.partial(advance, step), carry)
        if stop < nblk:
            CF[step] = carry[0]
            if step == 2:
                CQ[...] = carry[1]

    def pack_column():
        rolled = jnp.zeros((8, LANE), F32)
        lane8 = lax.broadcasted_iota(jnp.int32, (8, LANE), 1)
        sub8 = lax.broadcasted_iota(jnp.int32, (8, LANE), 0)

        def take(k, acc):
            cells = T[pl.ds(pl.multiple_of(EDGE + 8 * k, 8), 8), cols:width]
            cells = pltpu.roll(cells, (k + tx) % LANE, 1)
            return jnp.where(lane8 == k, cells, acc)

        rolled = lax.fori_loop(0, rows // 8, take, rolled)
        last = T[nrow - 8 : nrow, 0:LANE]
        T[nrow - 8 : nrow, 0:LANE] = jnp.where(sub8 == 0, last, rolled)
        last = T[nrow - 8 : nrow, LANE : 2 * LANE]
        T[nrow - 8 : nrow, LANE : 2 * LANE] = jnp.where(sub8 == 0, last, pltpu.roll(rolled, 1, 0))

    flying = {}
    sends = []

    def tile(k):
        r0 = sum(chunks[:k]) * R
        return r0, chunks[k] * R // 2

    def each(count, body):
        def loop(i, carry):
            body(pl.multiple_of(i * 8, 8))
            return carry

        lax.fori_loop(0, count // 8, loop, 0)

    def send(k, n, src, dst, peer):
        copy = remote(src, dst, ring_send.at[k, n], ring_recv.at[k, n], peer)
        flying[k, n] = copy
        sends.append(copy)

    def block(j):
        return pl.ds(pl.multiple_of(j * LANE, LANE), LANE)

    def piece(p):
        return pl.ds(pl.multiple_of(p * 2 * LANE, 2 * LANE), 2 * LANE)

    def stage0(k):
        r0, h = tile(k)
        h0 = r0 // 2
        theirs = pl.multiple_of(r0 + (1 - core) * h, 8)
        send(k, 0, T.at[pl.ds(theirs, h), 0:cols], CR.at[h0 : h0 + h], sibling)

    def stage1(k):
        r0, h = tile(k)
        h0 = r0 // 2
        mine = pl.multiple_of(r0 + core * h, 8)
        flying[k, 0].wait_recv()

        def body(i):
            at = pl.ds(h0 + i, 8)
            PP[at, :] = T[pl.ds(mine + i, 8), 0:cols] + CR[at, :]

        each(h, body)
        at = pl.ds(h0, h)
        send(k, 1, PP.at[at, block(2 * xf)], RAL.at[at], right)
        send(k, 2, PP.at[at, block(2 * xf + 1)], RAR.at[at], left)
        send(k, 3, PP.at[at, block(2 * xr + 1)], RBL.at[at], right)
        send(k, 4, PP.at[at, block(2 * xl)], RBR.at[at], left)

    def stage2(k):
        r0, h = tile(k)
        h0 = r0 // 2
        at = pl.ds(h0, h)
        flying[k, 1].wait_recv()

        def body1(i):
            at = pl.ds(h0 + i, 8)
            C1[at, :] = PP[at, block(2 * xr)] + RAL[at, :]

        each(h, body1)
        send(k, 5, C1.at[at], RCL.at[at], right)
        flying[k, 2].wait_recv()

        def body2(i):
            at = pl.ds(h0 + i, 8)
            C2[at, :] = PP[at, block(2 * xl + 1)] + RAR[at, :]

        each(h, body2)
        send(k, 6, C2.at[at], RCR.at[at], left)

    def stage3(k):
        r0, h = tile(k)
        h0 = r0 // 2
        at = pl.ds(h0, h)
        for n in (3, 4, 5, 6):
            flying[k, n].wait_recv()

        def body(i):
            at = pl.ds(h0 + i, 8)
            S[at, 0:LANE] = PP[at, block(2 * x)] + (RCL[at, :] + RBR[at, :])
            S[at, LANE : 2 * LANE] = PP[at, block(2 * x + 1)] + (RCR[at, :] + RBL[at, :])

        each(h, body)
        send(k, 7, S.at[at], RZ.at[at], zpeer)

    def stage4(k):
        r0, h = tile(k)
        h0 = r0 // 2
        mine = pl.multiple_of(r0 + core * h, 8)
        flying[k, 7].wait_recv()

        def body(i):
            at = pl.ds(h0 + i, 8)
            M[pl.ds(mine + i, 8), piece(x)] = S[at, :] + RZ[at, :]

        each(h, body)
        own = M.at[pl.ds(mine, h), piece(x)]
        send(k, 8, own, own, right)
        send(k, 9, own, own, left)
        send(k, 12, own, own, sibling)

    def stage5(k):
        r0, h = tile(k)
        mine = pl.multiple_of(r0 + core * h, 8)
        flying[k, 8].wait_recv()
        half = M.at[pl.ds(mine, h), block(2 * xl)]
        send(k, 10, half, half, right)
        flying[k, 9].wait_recv()
        half = M.at[pl.ds(mine, h), block(2 * xr + 1)]
        send(k, 11, half, half, left)
        for n, p in ((13, xl), (14, xr)):
            got = M.at[pl.ds(mine, h), piece(p)]
            send(k, n, got, got, sibling)

    def stage6(k):
        r0, h = tile(k)
        mine = pl.multiple_of(r0 + core * h, 8)
        flying[k, 10].wait_recv()
        flying[k, 11].wait_recv()
        got = M.at[pl.ds(mine, h), piece(xf)]
        send(k, 15, got, got, sibling)

    def stage7(k):
        for n in (12, 13, 14, 15):
            flying[k, n].wait_recv()

    stages = (stage0, stage1, stage2, stage3, stage4, stage5, stage6, stage7)
    at_stage = [0] * len(chunks)

    def progress(k):
        if at_stage[k] < len(stages):
            stages[at_stage[k]](k)
            at_stage[k] += 1

    for k in range(len(chunks)):
        stop = sum(chunks[: k + 1])
        run(0, stop + 2)
        run(1, stop + 1)
        run(2, stop)
        if k == len(chunks) - 1:
            pack_column()
        for j in range(k + 1):
            progress(j)
    state_copies = [
        pltpu.make_async_copy(field.at[EDGE : EDGE + rows, 0:cols], hy_h.at[0, i], out_sem.at[i])
        for i, field in enumerate((E, U, V))
    ]
    for copy in state_copies:
        copy.start()
    while min(at_stage) < len(stages):
        for k in range(len(chunks)):
            progress(k)

    change_copy = pltpu.make_async_copy(M.at[EDGE : EDGE + rows, 0:cols], bc_h, out_sem.at[3])
    change_copy.start()

    sub8 = lax.broadcasted_iota(jnp.int32, (8, LANE), 0)
    column = jnp.where(sub8 == 0, pltpu.roll(M[nrow - 8 : nrow, LANE : 2 * LANE], 7, 0), M[nrow - 8 : nrow, 0:LANE])

    def spread(k, carry):
        at = pl.ds(pl.multiple_of(EDGE + 8 * k, 8), 8)
        M[at, cols:width] = pltpu.roll(column, (2 * LANE - k - tx) % LANE, 1)
        return carry

    lax.fori_loop(0, rows // 8, spread, 0)

    place = lax.broadcasted_iota(jnp.int32, (R, width), 1)
    rows24 = lax.broadcasted_iota(jnp.int32, (R + 8, width), 0)
    inside_c = (place < cols) & (tx * cols + place <= ntx * cols - 2) | (place == width - 1) & (tx > 0)

    def bed_update(i, carry):
        r = pl.multiple_of(EDGE + i * R, 8)
        z = BED[pl.ds(r - 8, R + 16), :] + M[pl.ds(r - 8, R + 16), :]
        mid = z[8 : 8 + R]
        slope_c = jnp.where(inside_c, east(mid) - mid, 0.0)
        spill_c = 0.25 * (slope_c - jnp.clip(slope_c, -1.0, 1.0))
        top = z[: R + 8]
        at = rows24 + (ty * rows + i * R - 8)
        below_z = pltpu.roll(z, R + 15, 0)[: R + 8]
        slope_r = jnp.where((at >= 0) & (at <= nty * rows - 2), below_z - top, 0.0)
        spill_r = 0.25 * (slope_r - jnp.clip(slope_r, -1.0, 1.0))
        flow_r = (spill_r - pltpu.roll(spill_r, 1, 0))[8:]
        bed_new = mid + (spill_c - west(spill_c)) + flow_r
        BN[pl.ds(i * R, R), :] = bed_new[:, 0:cols]
        return carry

    lax.fori_loop(0, rows // R, bed_update, 0)
    bed_copy = pltpu.make_async_copy(BN, bn_h, out_sem.at[4])
    bed_copy.start()
    for copy in halo_copies + strip_copies + sends:
        copy.wait_send()
    for copy in state_copies:
        copy.wait()
    change_copy.wait()
    bed_copy.wait()


def shards(bed, land_mask, cell_class, weights, cond_params, wave_stress, hydro_state):
    rows, cols = bed.shape
    chunks = CHUNKS
    nrow, width = rows + 2 * EDGE, cols + LANE
    assert sum(chunks) * R == nrow
    half = nrow // 2
    vm = pltpu.VMEM
    full = vm((nrow, width), F32)
    tall = vm((nrow + 8, width), F32)
    ints = vm((nrow, width), jnp.int32)
    thin = vm((half, LANE), F32)
    dma = pltpu.SemaphoreType.DMA
    hbm = pl.BlockSpec(memory_space=pl.ANY)
    smem = pl.BlockSpec(memory_space=pltpu.SMEM)
    return pl.pallas_call(
        functools.partial(kernel, rows, cols, chunks),
        out_shape=(
            jax.ShapeDtypeStruct((rows, cols), F32),
            jax.ShapeDtypeStruct((rows, cols), F32),
            jax.ShapeDtypeStruct(hydro_state.shape, F32),
        ),
        in_specs=[hbm, hbm, hbm, smem, smem, hbm, hbm],
        out_specs=(hbm, hbm, hbm),
        scratch_shapes=[
            tall, full, full, full, full, full, ints, ints,
            tall, full, full, full, full, full, full, full, full,
            full, full, vm((rows, cols), F32),
            vm((3, 8, width), F32), vm((8, width), F32),
            vm((6, rows, LANE), F32), vm((2, rows, LANE), jnp.int32),
            vm((rows, LANE), F32), vm((nrow, LANE), F32),
            vm((half, cols), F32), vm((half, cols), F32),
            thin, thin, thin, thin, thin, thin, thin, thin,
            vm((half, 2 * LANE), F32), vm((half, 2 * LANE), F32),
            dma((8,)), dma((8,)), dma((2, 8)), dma((2, 8)), dma((3,)), dma((3,)),
            dma((len(chunks), 16)), dma((len(chunks), 16)), dma((5,)),
        ],
        compiler_params=pltpu.CompilerParams(
            collective_id=0, has_side_effects=True, vmem_limit_bytes=60 * 1024 * 1024
        ),
    )(bed, land_mask, cell_class, weights, cond_params, wave_stress, hydro_state)


def solution(mesh):
    in_specs = (
        P("ty", "tx"),
        P("ty", "tx"),
        P("ty", "tx"),
        P(),
        P("cond", None),
        P("cond", None, "ty", "tx"),
        P("cond", None, "ty", "tx"),
    )
    out_specs = (P("ty", "tx"), P("ty", "tx"), P("cond", None, "ty", "tx"))
    return jax.shard_map(shards, mesh=mesh, in_specs=in_specs, out_specs=out_specs, check_vma=False)
```

time: 354 us -> 68.4 us (0.19); the launches traced: 350 us -> 68.3 us
  waiting for transfers between devices: 171 us -> 0 us
  Pallas kernels: 0 us -> 61.2 us
  local copies, waits for them, and re-layouts: 66.4 us -> 6.43 us
  other arithmetic: 48.9 us -> 0 us
  starting transfers between devices: 45.4 us -> 0 us
  between operations: 18.2 us -> 0.65 us
    psum x1 -> x0, waiting for transfers between devices: 141 us -> none  [shards(): merged = lax.psum(term, 'cond')]
    pallas_call x0 -> x1, Pallas kernels: none -> 61.2 us  [shards(): pl.pallas_call(functools.partial(kernel, rows, cols, chunks), out_shape=(...]
    ppermute x20 -> x0, starting transfers between devices: 45.3 us -> none  [the longest x10 31.7 us: padded(): lax.ppermute(tail, axis, [(i, (i + 1) % count) for i in range(ends)])]
    ppermute x20 -> x0, waiting for transfers between devices: 29.9 us -> none  [the longest x10 23 us: padded(): lax.ppermute(head, axis, [((i + 1) % count, i) for i in range(ends)])]
    mul x15 -> x0, other arithmetic: 27.8 us -> none  [the longest x3 11.4 us: advance(): load_r = coef * wet_r * new_r * jnp.abs(new_r)]
    concatenate x6 -> x0, local copies, waits for them, and re-layouts: 25.6 us -> none  [the longest x5 25.4 us: padded(): jnp.concatenate([lax.ppermute(tail, axis, [(i, (i + 1) % count) for i in...]
    squeeze x5 -> x0, local copies, waits for them, and re-layouts: 14.1 us -> none  [the longest x3 7.13 us: shards(): widened[1]]
    another operation x4 -> x0, other arithmetic: 9.92 us -> none  [the longest x3 8.04 us: advance(): return (jnp.stack([new_level, new_c[1:-1, 1:], new_r[1:, 1:-1]]), delta)]
  transfers between devices with their start and end apart: 21 -> 0, of which waited for: 11 -> 0; matrix products, arithmetic and copies ran while one was open for 7% -> 0% of each run, Pallas kernels for 0% -> 0%
where the time goes in v1:
time: 68.4 us; the launch traced here: 68.3 us
  Pallas kernels  61.2 us (89%)
  local copies, waits for them, and re-layouts  6.43 us (9%)
    pallas_call x1, Pallas kernels, shards(): pl.pallas_call(functools.partial(kernel, rows, cols, chunks), out_shape=(...  61.2 us
    unnamed x5, local copies, waits for them, and re-layouts  6.43 us

profile of v1, /device:TPU:1, one launch (start us, length us, event | category | flops | bytes accessed | tf_op | source)
XLA Modules:
  0.0 68.3 jit_solution(16624727844095634685)
XLA Ops:
  0.6 61.2 %shard_map.94 = (f32[256,1024]{1,0:T(8,128)}, f32[256,1024]{1,0:T(8,128)}, f32[1,3,256,1024]{3,2,1,0:T(8,128)}) custom-call(f32[256,1024]{1,0:T(8,128)} %bed_h.1, s32[256,1024]{1,0:T(8,128)} %mask_h.1, s32[256,1024]{1,0:T(8,128)} %cls_h.1, s32[16]{0:T(128)} %wts.1, f32[1,4]{1,0:T(1,128)} %par.1, f32[1,2,256,1024]{3,2,1,0:T(8,128)} %stress_h.1, ...), custom_call_target="tpu_custom_call" | custom-call | tf_op jit(solution)/shard_map/pallas_call | solution.py:569
  61.8 0.0 copy-start
  61.8 2.5 %copy.13 = f32[256,1024]{1,0:T(8,128)} copy(f32[256,1024]{1,0:T(8,128)} %get-tuple-element.6) | data formatting | bytes 2097152
  64.3 2.3 %copy.14 = f32[256,1024]{1,0:T(8,128)} copy(f32[256,1024]{1,0:T(8,128)} %get-tuple-element.7) | data formatting | bytes 2097152
  66.6 0.0 copy-done
  66.6 1.7 %copy.15 = f32[1,3,256,1024]{3,2,1,0:T(8,128)} copy(f32[1,3,256,1024]{3,2,1,0:T(8,128)S(1)} %copy-done) | data formatting | bytes 6291456
Async XLA Ops:
  61.8 4.8 %copy-start = (f32[1,3,256,1024]{3,2,1,0:T(8,128)S(1)}, f32[1,3,256,1024]{3,2,1,0:T(8,128)}, u32[]{:S(2)}) copy-start(f32[1,3,256,1024]{3,2,1,0:T(8,128)} %get-tuple-element.8) | copy-start | bytes 9437188

commit v2 on v1

--- a/solution.py
+++ b/solution.py
@@ -12,15 +12,30 @@
 LANE = 128
 EDGE = 8
 HALO = 4
+GROUPS = 4
 R = 16
 NX = 4
-CHUNKS = (5, 4, 4, 4)
+FAR_FIRST = ((1, 2), (1, 1), (1, 3), (0, 2), (1, 0), (0, 1), (0, 3))
+PIN = True
+MERGE_VMEM = 56 << 20
+FINISH_VMEM = 16 << 20
+CHUNKS = (10, 7)
+SCHEDULE = ((10, (0,)), (13, (0,)), (17, (1, 0, 1, 0, 1)))
+
+
+def east(y):
+    return pltpu.roll(y, y.shape[1] - 1, 1)
+
+
+def west(y):
+    return pltpu.roll(y, 1, 1)
 
 
 def kernel(
     rows,
     cols,
     chunks,
+    schedule,
     bed_h,
     mask_h,
     cls_h,
@@ -28,15 +43,13 @@
     par,
     stress_h,
     hydro_h,
-    bn_h,
-    bc_h,
-    hy_h,
     E,
     U,
     V,
+    BED,
+    M,
     SX,
     SY,
-    BED,
     MASK,
     CLS,
     D,
@@ -49,8 +62,6 @@
     QC,
     QR,
     T,
-    M,
-    BN,
     CF,
     CQ,
     EDF,
@@ -59,16 +70,7 @@
     RSTRIP,
     CR,
     PP,
-    RAL,
-    RAR,
-    RBL,
-    RBR,
-    RCL,
-    RCR,
-    C1,
-    C2,
-    S,
-    RZ,
+    RX,
     in_sem,
     edge_sem,
     halo_send,
@@ -77,7 +79,6 @@
     strip_recv,
     ring_send,
     ring_recv,
-    out_sem,
 ):
     nrow = rows + 2 * EDGE
     width = cols + LANE
@@ -93,17 +94,15 @@
     up = (ty + nty - 1) % nty
     down = (ty + 1) % nty
     side = 1 - tx
-    xr = (x + 1) % NX
-    xl = (x + NX - 1) % NX
-    xf = (x + 2) % NX
 
     def cond_of(z, xx, k):
         return (z * NX + xx) * 2 + k
 
     sibling = (cond_of(zh, x, 1 - core), ty, tx)
-    right = (cond_of(zh, xr, core), ty, tx)
-    left = (cond_of(zh, xl, core), ty, tx)
-    zpeer = (cond_of(1 - zh, x, core), ty, tx)
+    chips = [((zh + dz) % 2, (x + dx) % NX) for dz, dx in FAR_FIRST]
+    partners = [(cond_of(z, xx, core), ty, tx) for z, xx in chips]
+    parts = [z * NX + xx for z, xx in chips]
+    own_part = zh * NX + x
     above = (c, up, tx)
     below = (c, down, tx)
     beside = (c, ty, side)
@@ -137,19 +136,16 @@
     for i in (5, 6, 0, 1, 2, 3, 4, 7):
         in_copies[i].start()
 
+    barrier = pltpu.get_barrier_semaphore()
+    peers = (sibling, *partners, above, below, beside, diag_up, diag_down)
+    for peer in peers:
+        pl.semaphore_signal(barrier, inc=1, device_id=peer, device_id_type=MESH)
     pad = EDGE - HALO
     for field in fields:
         field[0:pad, 0:cols] = jnp.zeros((pad, cols), field.dtype)
         field[nrow - pad : nrow, 0:cols] = jnp.zeros((pad, cols), field.dtype)
     E[nrow : nrow + 8, :] = jnp.zeros((8, width), F32)
     D[nrow : nrow + 8, :] = jnp.zeros((8, width), F32)
-    M[0:EDGE, cols:width] = jnp.zeros((EDGE, LANE), F32)
-    M[nrow - EDGE : nrow, cols:width] = jnp.zeros((EDGE, LANE), F32)
-
-    barrier = pltpu.get_barrier_semaphore()
-    peers = (sibling, right, left, zpeer, above, below, beside, diag_up, diag_down)
-    for peer in peers:
-        pl.semaphore_signal(barrier, inc=1, device_id=peer, device_id_type=MESH)
     pl.semaphore_wait(barrier, len(peers))
 
     def remote(src, dst, send, recv, peer):
@@ -184,21 +180,25 @@
     for copy in edge_copies:
         copy.wait()
 
+    group = rows // GROUPS
+
     def pack(i, carry):
-        r = pl.multiple_of(i * R, R)
         strip = jnp.zeros((R, LANE), F32)
-        for k in range(8):
-            cells = edges[k][pl.ds(r, R), :].astype(F32)
-            cells = pltpu.roll(cells, HALO * k + HALO * (1 - tx), 1)
-            strip = jnp.where((lanes >= HALO * k) & (lanes < HALO * (k + 1)), cells, strip)
-        PS[pl.ds(r, R), :] = strip
+        for g in range(GROUPS):
+            r = pl.multiple_of(g * group + i * R, R)
+            for k in range(8):
+                first = (g * 8 + k) * HALO
+                cells = edges[k][pl.ds(r, R), :].astype(F32)
+                cells = pltpu.roll(cells, (first + HALO * (1 - tx)) % LANE, 1)
+                strip = jnp.where((lanes >= first) & (lanes < first + HALO), cells, strip)
+        PS[pl.ds(pl.multiple_of(i * R, R), R), :] = strip
         return carry
 
-    lax.fori_loop(0, rows // R, pack, 0)
+    lax.fori_loop(0, group // R, pack, 0)
     strip_copies = [
-        remote(PS, RSTRIP.at[EDGE : EDGE + rows], strip_send.at[0], strip_recv.at[0], beside),
-        remote(PS.at[rows - 8 : rows], RSTRIP.at[0:8], strip_send.at[1], strip_recv.at[1], diag_down),
-        remote(PS.at[0:8], RSTRIP.at[nrow - 8 : nrow], strip_send.at[2], strip_recv.at[2], diag_up),
+        remote(PS, RSTRIP.at[8 : 8 + group], strip_send.at[0], strip_recv.at[0], beside),
+        remote(PS.at[group - 8 : group], RSTRIP.at[0:8], strip_send.at[1], strip_recv.at[1], diag_down),
+        remote(PS.at[0:8], RSTRIP.at[group + 8 : group + 16], strip_send.at[2], strip_recv.at[2], diag_up),
     ]
 
     def depth_of(mask, bed):
@@ -218,23 +218,29 @@
     for copy in strip_copies:
         copy.wait_recv()
 
-    row_ids = lax.broadcasted_iota(jnp.int32, (R, LANE), 0)
-
-    def unpack(i, carry):
-        r = pl.multiple_of(i * R, R)
-        strip = RSTRIP[pl.ds(r, R), :]
-        inner = (lanes < HALO) & (tx == 0) | (lanes >= LANE - HALO) & (tx == 1)
+    def unpack(n, src, dst, g, real):
+        strip = RSTRIP[pl.ds(src, n), :]
+        lane = lanes[:n]
+        inner = (lane < HALO) & (tx == 0) | (lane >= LANE - HALO) & (tx == 1)
+        at = pl.ds(dst, n)
+        parts = []
         for k in range(8):
-            shift = (LANE - HALO * k) * (1 - tx) + (LANE - HALO - HALO * k) * tx
+            shift = 2 * LANE - (g * 8 + k) * HALO - HALO * tx
             cells = jnp.where(inner, pltpu.roll(strip, shift % LANE, 1), 0.0)
-            fields[k][pl.ds(r, R), cols:width] = cells.astype(fields[k].dtype)
-        depth = depth_of(MASK[pl.ds(r, R), cols:width], BED[pl.ds(r, R), cols:width])
-        at = row_ids + r
-        real = ((at >= EDGE) | (ty > 0)) & ((at < EDGE + rows) | (ty < nty - 1))
-        D[pl.ds(r, R), cols:width] = jnp.where(real, depth, 0.0)
+            parts.append(cells.astype(fields[k].dtype))
+            fields[k][at, cols:width] = parts[k]
+        depth = depth_of(parts[6], parts[5])
+        D[at, cols:width] = depth if real is None else jnp.where(real, depth, 0.0)
+
+    def unpack_rows(i, carry):
+        for g in range(GROUPS):
+            r = pl.multiple_of(i * R, R)
+            unpack(R, 8 + r, pl.multiple_of(EDGE + g * group + r, 8), g, None)
         return carry
 
-    lax.fori_loop(0, nblk, unpack, 0)
+    lax.fori_loop(0, group // R, unpack_rows, 0)
+    unpack(8, 0, 0, GROUPS - 1, ty > 0)
+    unpack(8, group + 8, nrow - 8, 0, ty < nty - 1)
     wide_rows = lax.broadcasted_iota(jnp.int32, (R, cols), 0)
     for r in (0, nrow - R):
         depth = depth_of(MASK[r : r + R, 0:cols], BED[r : r + R, 0:cols])
@@ -261,12 +267,6 @@
 
     def north(before, y):
         return pltpu.roll(jnp.concatenate([before, y], axis=0), 1, 0)[8:]
-
-    def east(y):
-        return pltpu.roll(y, width - 1, 1)
-
-    def west(y):
-        return pltpu.roll(y, 1, 1)
 
     def advance(step, i, carry):
         r = pl.multiple_of(i * R, R)
@@ -350,7 +350,7 @@
             cells = pltpu.roll(cells, (k + tx) % LANE, 1)
             return jnp.where(lane8 == k, cells, acc)
 
-        rolled = lax.fori_loop(0, rows // 8, take, rolled)
+        rolled = lax.fori_loop(0, rows // 8, take, rolled, unroll=8)
         last = T[nrow - 8 : nrow, 0:LANE]
         T[nrow - 8 : nrow, 0:LANE] = jnp.where(sub8 == 0, last, rolled)
         last = T[nrow - 8 : nrow, LANE : 2 * LANE]
@@ -377,9 +377,6 @@
 
     def block(j):
         return pl.ds(pl.multiple_of(j * LANE, LANE), LANE)
-
-    def piece(p):
-        return pl.ds(pl.multiple_of(p * 2 * LANE, 2 * LANE), 2 * LANE)
 
     def stage0(k):
         r0, h = tile(k)
@@ -399,89 +396,40 @@
 
         each(h, body)
         at = pl.ds(h0, h)
-        send(k, 1, PP.at[at, block(2 * xf)], RAL.at[at], right)
-        send(k, 2, PP.at[at, block(2 * xf + 1)], RAR.at[at], left)
-        send(k, 3, PP.at[at, block(2 * xr + 1)], RBL.at[at], right)
-        send(k, 4, PP.at[at, block(2 * xl)], RBR.at[at], left)
+        for n, partner in enumerate(partners):
+            send(k, 1 + n, PP.at[at, block(parts[n])], RX.at[n, at], partner)
 
     def stage2(k):
         r0, h = tile(k)
         h0 = r0 // 2
-        at = pl.ds(h0, h)
-        flying[k, 1].wait_recv()
-
-        def body1(i):
+        mine = pl.multiple_of(r0 + core * h, 8)
+        for n in range(len(partners)):
+            flying[k, 1 + n].wait_recv()
+
+        def body(i):
             at = pl.ds(h0 + i, 8)
-            C1[at, :] = PP[at, block(2 * xr)] + RAL[at, :]
-
-        each(h, body1)
-        send(k, 5, C1.at[at], RCL.at[at], right)
-        flying[k, 2].wait_recv()
-
-        def body2(i):
-            at = pl.ds(h0 + i, 8)
-            C2[at, :] = PP[at, block(2 * xl + 1)] + RAR[at, :]
-
-        each(h, body2)
-        send(k, 6, C2.at[at], RCR.at[at], left)
+            acc = PP[at, block(own_part)]
+            for n in range(len(partners)):
+                acc = acc + RX[n, at, :]
+            M[pl.ds(mine + i, 8), block(own_part)] = acc
+
+        each(h, body)
+        own = M.at[pl.ds(mine, h), block(own_part)]
+        for n, partner in enumerate(partners):
+            send(k, 8 + n, own, own, partner)
 
     def stage3(k):
         r0, h = tile(k)
-        h0 = r0 // 2
-        at = pl.ds(h0, h)
-        for n in (3, 4, 5, 6):
-            flying[k, n].wait_recv()
-
-        def body(i):
-            at = pl.ds(h0 + i, 8)
-            S[at, 0:LANE] = PP[at, block(2 * x)] + (RCL[at, :] + RBR[at, :])
-            S[at, LANE : 2 * LANE] = PP[at, block(2 * x + 1)] + (RCR[at, :] + RBL[at, :])
-
-        each(h, body)
-        send(k, 7, S.at[at], RZ.at[at], zpeer)
+        mine = pl.multiple_of(r0 + core * h, 8)
+        for n in range(len(partners)):
+            flying[k, 8 + n].wait_recv()
+        got = M.at[pl.ds(mine, h), 0:cols]
+        send(k, 15, got, got, sibling)
 
     def stage4(k):
-        r0, h = tile(k)
-        h0 = r0 // 2
-        mine = pl.multiple_of(r0 + core * h, 8)
-        flying[k, 7].wait_recv()
-
-        def body(i):
-            at = pl.ds(h0 + i, 8)
-            M[pl.ds(mine + i, 8), piece(x)] = S[at, :] + RZ[at, :]
-
-        each(h, body)
-        own = M.at[pl.ds(mine, h), piece(x)]
-        send(k, 8, own, own, right)
-        send(k, 9, own, own, left)
-        send(k, 12, own, own, sibling)
-
-    def stage5(k):
-        r0, h = tile(k)
-        mine = pl.multiple_of(r0 + core * h, 8)
-        flying[k, 8].wait_recv()
-        half = M.at[pl.ds(mine, h), block(2 * xl)]
-        send(k, 10, half, half, right)
-        flying[k, 9].wait_recv()
-        half = M.at[pl.ds(mine, h), block(2 * xr + 1)]
-        send(k, 11, half, half, left)
-        for n, p in ((13, xl), (14, xr)):
-            got = M.at[pl.ds(mine, h), piece(p)]
-            send(k, n, got, got, sibling)
-
-    def stage6(k):
-        r0, h = tile(k)
-        mine = pl.multiple_of(r0 + core * h, 8)
-        flying[k, 10].wait_recv()
-        flying[k, 11].wait_recv()
-        got = M.at[pl.ds(mine, h), piece(xf)]
-        send(k, 15, got, got, sibling)
-
-    def stage7(k):
-        for n in (12, 13, 14, 15):
-            flying[k, n].wait_recv()
-
-    stages = (stage0, stage1, stage2, stage3, stage4, stage5, stage6, stage7)
+        flying[k, 15].wait_recv()
+
+    stages = (stage0, stage1, stage2, stage3, stage4)
     at_stage = [0] * len(chunks)
 
     def progress(k):
@@ -489,37 +437,48 @@
             stages[at_stage[k]](k)
             at_stage[k] += 1
 
-    for k in range(len(chunks)):
-        stop = sum(chunks[: k + 1])
+    for stop, ready in schedule:
         run(0, stop + 2)
         run(1, stop + 1)
         run(2, stop)
-        if k == len(chunks) - 1:
+        if stop == nblk:
             pack_column()
-        for j in range(k + 1):
-            progress(j)
-    state_copies = [
+        for k in ready:
+            progress(k)
+    while min(at_stage) < len(stages):
+        for k in range(len(chunks)):
+            progress(k)
+
+    for copy in halo_copies + strip_copies + sends:
+        copy.wait_send()
+
+
+def finish(rows, cols, E, U, V, BED, M, bn_h, bc_h, hy_h, Z, BN, out_sem):
+    nrow = rows + 2 * EDGE
+    width = cols + LANE
+    ty = lax.axis_index("ty")
+    tx = lax.axis_index("tx")
+    nty = lax.axis_size("ty")
+    ntx = lax.axis_size("tx")
+    copies = [
         pltpu.make_async_copy(field.at[EDGE : EDGE + rows, 0:cols], hy_h.at[0, i], out_sem.at[i])
         for i, field in enumerate((E, U, V))
     ]
-    for copy in state_copies:
+    copies.append(pltpu.make_async_copy(M.at[EDGE : EDGE + rows, 0:cols], bc_h, out_sem.at[3]))
+    for copy in copies:
         copy.start()
-    while min(at_stage) < len(stages):
-        for k in range(len(chunks)):
-            progress(k)
-
-    change_copy = pltpu.make_async_copy(M.at[EDGE : EDGE + rows, 0:cols], bc_h, out_sem.at[3])
-    change_copy.start()
 
     sub8 = lax.broadcasted_iota(jnp.int32, (8, LANE), 0)
     column = jnp.where(sub8 == 0, pltpu.roll(M[nrow - 8 : nrow, LANE : 2 * LANE], 7, 0), M[nrow - 8 : nrow, 0:LANE])
 
     def spread(k, carry):
         at = pl.ds(pl.multiple_of(EDGE + 8 * k, 8), 8)
-        M[at, cols:width] = pltpu.roll(column, (2 * LANE - k - tx) % LANE, 1)
+        Z[at, :] = pltpu.roll(column, (2 * LANE - k - tx) % LANE, 1)
         return carry
 
-    lax.fori_loop(0, rows // 8, spread, 0)
+    Z[0:EDGE, :] = jnp.zeros((EDGE, LANE), F32)
+    Z[nrow - EDGE : nrow, :] = jnp.zeros((EDGE, LANE), F32)
+    lax.fori_loop(0, rows // 8, spread, 0, unroll=8)
 
     place = lax.broadcasted_iota(jnp.int32, (R, width), 1)
     rows24 = lax.broadcasted_iota(jnp.int32, (R + 8, width), 0)
@@ -527,7 +486,8 @@
 
     def bed_update(i, carry):
         r = pl.multiple_of(EDGE + i * R, 8)
-        z = BED[pl.ds(r - 8, R + 16), :] + M[pl.ds(r - 8, R + 16), :]
+        at = pl.ds(r - 8, R + 16)
+        z = BED[at, :] + jnp.concatenate([M[at, :], Z[at, :]], axis=1)
         mid = z[8 : 8 + R]
         slope_c = jnp.where(inside_c, east(mid) - mid, 0.0)
         spill_c = 0.25 * (slope_c - jnp.clip(slope_c, -1.0, 1.0))
@@ -542,14 +502,14 @@
         return carry
 
     lax.fori_loop(0, rows // R, bed_update, 0)
-    bed_copy = pltpu.make_async_copy(BN, bn_h, out_sem.at[4])
-    bed_copy.start()
-    for copy in halo_copies + strip_copies + sends:
-        copy.wait_send()
-    for copy in state_copies:
+    copies.append(pltpu.make_async_copy(BN, bn_h, out_sem.at[4]))
+    copies[-1].start()
+    for copy in copies:
         copy.wait()
-    change_copy.wait()
-    bed_copy.wait()
+
+
+def pinned(ref):
+    return ref if PIN else jax.ShapeDtypeStruct(ref.shape, ref.dtype)
 
 
 def shards(bed, land_mask, cell_class, weights, cond_params, wave_stress, hydro_state):
@@ -562,36 +522,46 @@
     full = vm((nrow, width), F32)
     tall = vm((nrow + 8, width), F32)
     ints = vm((nrow, width), jnp.int32)
-    thin = vm((half, LANE), F32)
     dma = pltpu.SemaphoreType.DMA
-    hbm = pl.BlockSpec(memory_space=pl.ANY)
+    hbm = pl.BlockSpec(memory_space=pltpu.HBM)
     smem = pl.BlockSpec(memory_space=pltpu.SMEM)
+    vmem = pl.BlockSpec(memory_space=pltpu.VMEM)
+    merge = pl.pallas_call(
+        functools.partial(kernel, rows, cols, chunks, SCHEDULE),
+        out_shape=tuple(pinned(ref) for ref in (tall, full, full, full, vm((nrow, cols), F32))),
+        in_specs=[hbm, hbm, hbm, smem, smem, hbm, hbm],
+        out_specs=(vmem,) * 5,
+        scratch_shapes=[
+            full, full, ints, ints,
+            tall, full, full, full, full, full, full, full, full, full,
+            vm((3, 8, width), F32), vm((8, width), F32),
+            vm((6, rows, LANE), F32), vm((2, rows, LANE), jnp.int32),
+            vm((rows // GROUPS, LANE), F32), vm((rows // GROUPS + 16, LANE), F32),
+            vm((half, cols), F32), vm((half, cols), F32), vm((7, half, LANE), F32),
+            dma((8,)), dma((8,)), dma((2, 8)), dma((2, 8)), dma((3,)), dma((3,)),
+            dma((len(chunks), 16)), dma((len(chunks), 16)),
+        ],
+        compiler_params=pltpu.CompilerParams(
+            collective_id=0, has_side_effects=True, vmem_limit_bytes=MERGE_VMEM
+        ),
+        name="merge",
+    )
+    fields = merge(bed, land_mask, cell_class, weights, cond_params, wave_stress, hydro_state)
+    if PIN:
+        fields = [pltpu.with_memory_space_constraint(field, pltpu.VMEM) for field in fields]
     return pl.pallas_call(
-        functools.partial(kernel, rows, cols, chunks),
+        functools.partial(finish, rows, cols),
         out_shape=(
             jax.ShapeDtypeStruct((rows, cols), F32),
             jax.ShapeDtypeStruct((rows, cols), F32),
             jax.ShapeDtypeStruct(hydro_state.shape, F32),
         ),
-        in_specs=[hbm, hbm, hbm, smem, smem, hbm, hbm],
+        in_specs=[vmem] * 5,
         out_specs=(hbm, hbm, hbm),
-        scratch_shapes=[
-            tall, full, full, full, full, full, ints, ints,
-            tall, full, full, full, full, full, full, full, full,
-            full, full, vm((rows, cols), F32),
-            vm((3, 8, width), F32), vm((8, width), F32),
-            vm((6, rows, LANE), F32), vm((2, rows, LANE), jnp.int32),
-            vm((rows, LANE), F32), vm((nrow, LANE), F32),
-            vm((half, cols), F32), vm((half, cols), F32),
-            thin, thin, thin, thin, thin, thin, thin, thin,
-            vm((half, 2 * LANE), F32), vm((half, 2 * LANE), F32),
-            dma((8,)), dma((8,)), dma((2, 8)), dma((2, 8)), dma((3,)), dma((3,)),
-            dma((len(chunks), 16)), dma((len(chunks), 16)), dma((5,)),
-        ],
-        compiler_params=pltpu.CompilerParams(
-            collective_id=0, has_side_effects=True, vmem_limit_bytes=60 * 1024 * 1024
-        ),
-    )(bed, land_mask, cell_class, weights, cond_params, wave_stress, hydro_state)
+        scratch_shapes=[vm((nrow, LANE), F32), vm((rows, cols), F32), dma((5,))],
+        compiler_params=pltpu.CompilerParams(vmem_limit_bytes=FINISH_VMEM),
+        name="finish",
+    )(*fields)
 
 
 def solution(mesh):

time: 68.4 us -> 50.9 us (0.74)
  Pallas kernels: 61.2 us -> 50.1 us
  local copies, waits for them, and re-layouts: 6.43 us -> 0 us
    pallas_call x1 -> x2, Pallas kernels: 61.2 us -> 50.1 us  [the longest x1 46 us: shards(): merge(bed, land_mask, cell_class, weights, cond_params, wave_stress, hydr...]
    unnamed x5 -> x0, local copies, waits for them, and re-layouts: 6.43 us -> none
where the time goes in v2:
time: 50.9 us; the launch traced here: 50.7 us
  Pallas kernels  50.1 us (98%)
  between operations  0.64 us (1%)
    pallas_call x1, Pallas kernels, shards(): merge(bed, land_mask, cell_class, weights, cond_params, wave_stress, hydr...  46 us
    pallas_call x1, Pallas kernels, shards(): pl.pallas_call(functools.partial(finish, rows, cols), out_shape=(jax.Shap...  4.08 us

profile of v2, /device:TPU:1, one launch (start us, length us, event | category | flops | bytes accessed | tf_op | source)
XLA Modules:
  0.0 50.7 jit_solution(3211467717833002938)
XLA Ops:
  0.6 46.0 %merge.1 = (f32[280,1152]{1,0:T(8,128)S(1)}, f32[272,1152]{1,0:T(8,128)S(1)}, f32[272,1152]{1,0:T(8,128)S(1)}, f32[272,1152]{1,0:T(8,128)S(1)}, f32[272,1024]{1,0:T(8,128)S(1)}) custom-call(f32[256,1024]{1,0:T(8,128)} %bed_h.1, s32[256,1024]{1,0:T(8,128)} %mask_h.1, s32[256,1024]{1,0:T(8,128)} %cls_h.1, s32[16]{0:T(128)} %wts.1, f32[1,4]{1,0:T(1,128)} %par.1, ...), custom_call_target="tpu_custom_call" | custom-call | tf_op jit(solution)/shard_map/merge/pallas_call | solution.py:549
  46.7 4.1 %finish.1 = (f32[256,1024]{1,0:T(8,128)}, f32[256,1024]{1,0:T(8,128)}, f32[1,3,256,1024]{3,2,1,0:T(8,128)}) custom-call(f32[280,1152]{1,0:T(8,128)S(1)} %get-tuple-element.8.E, f32[272,1152]{1,0:T(8,128)S(1)} %get-tuple-element.9.U, f32[272,1152]{1,0:T(8,128)S(1)} %get-tuple-element.10.V, f32[272,1152]{1,0:T(8,128)S(1)} %get-tuple-element.11.BED, ...), custom_call_target="tpu_custom_call" | custom-call | tf_op jit(solution)/shard_map/finish/pallas_call | solution.py:552

commit v3 on v2

--- a/solution.py
+++ b/solution.py
@@ -16,11 +16,12 @@
 R = 16
 NX = 4
 FAR_FIRST = ((1, 2), (1, 1), (1, 3), (0, 2), (1, 0), (0, 1), (0, 3))
+SKEW = 2
 PIN = True
 MERGE_VMEM = 56 << 20
 FINISH_VMEM = 16 << 20
 CHUNKS = (10, 7)
-SCHEDULE = ((10, (0,)), (13, (0,)), (17, (1, 0, 1, 0, 1)))
+SCHEDULE = ((10, (0,)), (13, (0,)), (17, (1, 1, 0, 1, 0, 1, 0, 1)))
 
 
 def east(y):
@@ -39,15 +40,24 @@
     bed_h,
     mask_h,
     cls_h,
-    wts,
-    par,
+    wts_h,
+    par_h,
     stress_h,
     hydro_h,
-    E,
-    U,
-    V,
+    E3,
+    U3,
+    V3,
     BED,
     M,
+    E,
+    E1,
+    E2,
+    U,
+    U1,
+    U2,
+    V,
+    V1,
+    V2,
     SX,
     SY,
     MASK,
@@ -60,7 +70,9 @@
     A,
     B,
     QC,
+    QC1,
     QR,
+    QR1,
     T,
     CF,
     CQ,
@@ -71,6 +83,9 @@
     CR,
     PP,
     RX,
+    wts,
+    par,
+    small_sem,
     in_sem,
     edge_sem,
     halo_send,
@@ -123,6 +138,12 @@
     edge_at = pl.multiple_of((1 - tx) * (cols - LANE), LANE)
     edges = [EDF.at[i] for i in range(6)] + [EDI.at[i] for i in range(2)]
 
+    small_copies = [
+        pltpu.make_async_copy(wts_h, wts, small_sem.at[0]),
+        pltpu.make_async_copy(par_h, par, small_sem.at[1]),
+    ]
+    for copy in small_copies:
+        copy.start()
     edge_copies = [
         pltpu.make_async_copy(src.at[:, pl.ds(edge_at, LANE)], dst, edge_sem.at[i])
         for i, (src, dst) in enumerate(zip(sources, edges))
@@ -144,7 +165,8 @@
     for field in fields:
         field[0:pad, 0:cols] = jnp.zeros((pad, cols), field.dtype)
         field[nrow - pad : nrow, 0:cols] = jnp.zeros((pad, cols), field.dtype)
-    E[nrow : nrow + 8, :] = jnp.zeros((8, width), F32)
+    for level in (E, E1, E2):
+        level[nrow : nrow + 8, :] = jnp.zeros((8, width), F32)
     D[nrow : nrow + 8, :] = jnp.zeros((8, width), F32)
     pl.semaphore_wait(barrier, len(peers))
 
@@ -208,11 +230,45 @@
     in_copies[6].wait()
 
     def depth_inner(i, carry):
-        r = pl.multiple_of(i * R, R)
-        D[pl.ds(r, R), 0:cols] = depth_of(MASK[pl.ds(r, R), 0:cols], BED[pl.ds(r, R), 0:cols])
+        at = pl.ds(pl.multiple_of(EDGE + i * R, 8), R)
+        D[at, 0:cols] = depth_of(MASK[at, 0:cols], BED[at, 0:cols])
         return carry
 
-    lax.fori_loop(1, nblk - 1, depth_inner, 0)
+    lax.fori_loop(0, rows // R, depth_inner, 0)
+
+    for copy in small_copies:
+        copy.wait()
+    in_copies[7].wait()
+    tide = par[0, 0] - 1.0
+    fric = 0.2 * par[0, 1]
+    coef = par[0, 2]
+    flow_in = 0.3 * par[0, 3]
+    keep = 1.0 - fric
+
+    def faces(depth, beyond, face, wet, at, span):
+        root = jnp.sqrt(depth * beyond)
+        wet[at, span] = root / (root + 0.1)
+        face[at, span] = 0.3 * root
+
+    def level_terms(depth, at, span):
+        kind = CLS[at, span]
+        relax = jnp.where(kind == 1, 0.5 * depth, 0.0)
+        A[at, span] = 0.3 * (relax * tide + flow_in * jnp.where(kind == 2, depth, 0.0))
+        B[at, span] = 1.0 - relax
+
+    def prepare(r, n, span):
+        at = pl.ds(r, n)
+        deep = D[pl.ds(r, n + 8), span]
+        depth = deep[:n]
+        faces(depth, east(depth), FC, WC, at, span)
+        faces(depth, pltpu.roll(deep, n + 7, 0)[:n], FR, WR, at, span)
+        level_terms(depth, at, span)
+
+    def prepare_inner(i, carry):
+        prepare(pl.multiple_of(i * R, R), R, slice(0, cols))
+        return carry
+
+    lax.fori_loop(1, nblk - 1, prepare_inner, 0)
     for copy in halo_copies:
         copy.wait_recv()
     for copy in strip_copies:
@@ -241,21 +297,30 @@
     lax.fori_loop(0, group // R, unpack_rows, 0)
     unpack(8, 0, 0, GROUPS - 1, ty > 0)
     unpack(8, group + 8, nrow - 8, 0, ty < nty - 1)
-    wide_rows = lax.broadcasted_iota(jnp.int32, (R, cols), 0)
+    for r, real in ((0, ty > 0), (nrow - 8, ty < nty - 1)):
+        depth = depth_of(MASK[r : r + 8, 0:cols], BED[r : r + 8, 0:cols])
+        D[r : r + 8, 0:cols] = jnp.where(real, depth, 0.0)
     for r in (0, nrow - R):
-        depth = depth_of(MASK[r : r + R, 0:cols], BED[r : r + R, 0:cols])
-        at = wide_rows + r
-        real = ((at >= EDGE) | (ty > 0)) & ((at < EDGE + rows) | (ty < nty - 1))
-        D[r : r + R, 0:cols] = jnp.where(real, depth, 0.0)
-
-    for i in (0, 1, 2, 3, 4, 7):
+        prepare(r, R, slice(0, width))
+
+    tall_block = (nblk - 2) * R // 3
+
+    def prepare_edge(i, carry):
+        r = pl.multiple_of(R + i * tall_block, R)
+        at = pl.ds(r, tall_block)
+        depth = D[at, cols - LANE : width]
+        beyond = east(jnp.concatenate([depth, D[at, 0:LANE]], axis=1))[:, : 2 * LANE]
+        faces(depth, beyond, FC, WC, at, slice(cols - LANE, width))
+        deep = D[pl.ds(r, tall_block + 8), cols:width]
+        span = slice(cols, width)
+        faces(deep[:tall_block], pltpu.roll(deep, tall_block + 7, 0)[:tall_block], FR, WR, at, span)
+        level_terms(deep[:tall_block], at, span)
+        return carry
+
+    lax.fori_loop(0, 3, prepare_edge, 0)
+    for i in range(5):
         in_copies[i].wait()
 
-    tide = par[0, 0] - 1.0
-    fric = 0.2 * par[0, 1]
-    coef = par[0, 2]
-    flow_in = 0.3 * par[0, 3]
-    keep = 1.0 - fric
     total = wts[0]
     for i in range(1, 16):
         total = total + wts[i]
@@ -268,77 +333,77 @@
     def north(before, y):
         return pltpu.roll(jnp.concatenate([before, y], axis=0), 1, 0)[8:]
 
-    def advance(step, i, carry):
-        r = pl.multiple_of(i * R, R)
+    levels, cols_vel, rows_vel = (E, E1, E2, E3), (U, U1, U2, U3), (V, V1, V2, V3)
+    cols_sum, rows_sum = (QC, QC1), (QR, QR1)
+
+    def beyond(step, r):
+        level = levels[step][pl.ds(r, R), :]
+        return east(0.3 * level if step == 0 else level)
+
+    def advance(step, r, ahead):
         here = pl.ds(r, R)
-        level = E[pl.ds(r, R + 8), :]
+        level = levels[step][pl.ds(r, R + 8), :]
         if step == 0:
             level = 0.3 * level
-            deep = D[pl.ds(r, R + 8), :]
-            depth = deep[:R]
-            face_c = jnp.sqrt(depth * east(depth))
-            face_r = jnp.sqrt(depth * south(deep))
-            wet_c = face_c / (face_c + 0.1)
-            wet_r = face_r / (face_r + 0.1)
-            face_c = 0.3 * face_c
-            face_r = 0.3 * face_r
-            kind = CLS[here, :]
-            relax = jnp.where(kind == 1, 0.5 * depth, 0.0)
-            add = 0.3 * (relax * tide + flow_in * jnp.where(kind == 2, depth, 0.0))
-            stay = 1.0 - relax
-            WC[here, :] = wet_c
-            WR[here, :] = wet_r
-            FC[here, :] = face_c
-            FR[here, :] = face_r
-            A[here, :] = add
-            B[here, :] = stay
-        else:
-            wet_c = WC[here, :]
-            wet_r = WR[here, :]
-            face_c = FC[here, :]
-            face_r = FR[here, :]
-            add = A[here, :]
-            stay = B[here, :]
+        wet_c = WC[here, :]
+        wet_r = WR[here, :]
+        face_c = FC[here, :]
+        face_r = FR[here, :]
         mid = level[:R]
-        vel_c = (keep * U[here, :] - (east(mid) - mid) + SX[here, :]) * wet_c
-        vel_r = (keep * V[here, :] - (south(level) - mid) + SY[here, :]) * wet_r
-        U[here, :] = vel_c
-        V[here, :] = vel_r
+        vel_c = (keep * cols_vel[step][here, :] - (ahead - mid) + SX[here, :]) * wet_c
+        vel_r = (keep * rows_vel[step][here, :] - (south(level) - mid) + SY[here, :]) * wet_r
+        cols_vel[step + 1][here, :] = vel_c
+        rows_vel[step + 1][here, :] = vel_r
         flux_c = face_c * vel_c
         flux_r = face_r * vel_r
-        level = mid * stay + add - (flux_c - west(flux_c)) - (flux_r - north(carry[0], flux_r))
+        level = mid * B[here, :] + A[here, :] - (flux_c - west(flux_c)) - (flux_r - north(CF[step], flux_r))
         if step == 2:
             level = level * (1.0 / 0.3)
-        E[here, :] = level
-        load_c = wet_c * vel_c * jnp.abs(vel_c)
-        load_r = wet_r * vel_r * jnp.abs(vel_r)
+        levels[step + 1][here, :] = level
+        load_c = vel_c * jnp.abs(vel_c)
+        load_r = vel_r * jnp.abs(vel_r)
         if step > 0:
-            load_c = load_c + QC[here, :]
-            load_r = load_r + QR[here, :]
+            load_c = load_c + cols_sum[step - 1][here, :]
+            load_r = load_r + rows_sum[step - 1][here, :]
         if step < 2:
-            QC[here, :] = load_c
-            QR[here, :] = load_r
-            return (flux_r[R - 8 :],)
-        T[here, :] = scale * (load_c - west(load_c) + load_r - north(carry[1], load_r))
-        return (flux_r[R - 8 :], load_r[R - 8 :])
-
+            cols_sum[step][here, :] = load_c
+            rows_sum[step][here, :] = load_r
+            CF[step] = flux_r[R - 8 :]
+            return
+        load_c = wet_c * load_c
+        load_r = wet_r * load_r
+        T[here, :] = scale * (load_c - west(load_c) + load_r - north(CQ[...], load_r))
+        CF[step] = flux_r[R - 8 :]
+        CQ[...] = load_r[R - 8 :]
+
+    CF[...] = jnp.zeros((3, 8, width), F32)
+    CQ[...] = jnp.zeros((8, width), F32)
     done = [0, 0, 0]
 
-    def run(step, stop):
-        stop = min(stop, nblk)
-        start = done[step]
-        if stop <= start:
+    def sweep(steps, count):
+        if count <= 0:
             return
-        done[step] = stop
-        if start == 0:
-            carry = (jnp.zeros((8, width), F32),) * (2 if step == 2 else 1)
-        else:
-            carry = (CF[step],) + ((CQ[...],) if step == 2 else ())
-        carry = lax.fori_loop(start, stop, functools.partial(advance, step), carry)
-        if stop < nblk:
-            CF[step] = carry[0]
-            if step == 2:
-                CQ[...] = carry[1]
+        starts = [done[step] for step in steps]
+
+        def body(i, carry):
+            r = pl.multiple_of(i * R, R)
+            places = [r + start * R for start in starts]
+            ahead = [beyond(step, place) for step, place in zip(steps, places)]
+            for step, place, cells in zip(steps, places, ahead):
+                advance(step, place, cells)
+            return carry
+
+        lax.fori_loop(0, count, body, 0)
+        for step in steps:
+            done[step] += count
+
+    def run(stop):
+        goals = [min(stop + SKEW * (2 - step), nblk) for step in range(3)]
+        sweep((0,), min(done[2] + 2 * SKEW, nblk) - done[0])
+        sweep((1,), min(done[2] + SKEW, nblk) - done[1])
+        sweep((0, 1, 2), goals[0] - done[0])
+        sweep((1, 2), goals[1] - done[1])
+        sweep((2,), goals[2] - done[2])
 
     def pack_column():
         rolled = jnp.zeros((8, LANE), F32)
@@ -438,9 +503,7 @@
             at_stage[k] += 1
 
     for stop, ready in schedule:
-        run(0, stop + 2)
-        run(1, stop + 1)
-        run(2, stop)
+        run(stop)
         if stop == nblk:
             pack_column()
         for k in ready:
@@ -498,12 +561,15 @@
         spill_r = 0.25 * (slope_r - jnp.clip(slope_r, -1.0, 1.0))
         flow_r = (spill_r - pltpu.roll(spill_r, 1, 0))[8:]
         bed_new = mid + (spill_c - west(spill_c)) + flow_r
-        BN[pl.ds(i * R, R), :] = bed_new[:, 0:cols]
+        BN[pl.ds(pl.multiple_of(i * R, R), R), :] = bed_new[:, 0:cols]
         return carry
 
-    lax.fori_loop(0, rows // R, bed_update, 0)
-    copies.append(pltpu.make_async_copy(BN, bn_h, out_sem.at[4]))
-    copies[-1].start()
+    parts = rows // R // 4
+    for part in range(4):
+        lax.fori_loop(part * parts, (part + 1) * parts, bed_update, 0)
+        at = slice(part * parts * R, (part + 1) * parts * R)
+        copies.append(pltpu.make_async_copy(BN.at[at], bn_h.at[at], out_sem.at[4 + part]))
+        copies[-1].start()
     for copy in copies:
         copy.wait()
 
@@ -524,20 +590,20 @@
     ints = vm((nrow, width), jnp.int32)
     dma = pltpu.SemaphoreType.DMA
     hbm = pl.BlockSpec(memory_space=pltpu.HBM)
-    smem = pl.BlockSpec(memory_space=pltpu.SMEM)
     vmem = pl.BlockSpec(memory_space=pltpu.VMEM)
     merge = pl.pallas_call(
         functools.partial(kernel, rows, cols, chunks, SCHEDULE),
-        out_shape=tuple(pinned(ref) for ref in (tall, full, full, full, vm((nrow, cols), F32))),
-        in_specs=[hbm, hbm, hbm, smem, smem, hbm, hbm],
+        out_shape=tuple(pinned(ref) for ref in (full, full, full, full, vm((nrow, cols), F32))),
+        in_specs=[hbm] * 7,
         out_specs=(vmem,) * 5,
         scratch_shapes=[
-            full, full, ints, ints,
-            tall, full, full, full, full, full, full, full, full, full,
+            tall, tall, tall, full, full, full, full, full, full, full, full, ints, ints,
+            tall, *[full] * 11,
             vm((3, 8, width), F32), vm((8, width), F32),
             vm((6, rows, LANE), F32), vm((2, rows, LANE), jnp.int32),
             vm((rows // GROUPS, LANE), F32), vm((rows // GROUPS + 16, LANE), F32),
             vm((half, cols), F32), vm((half, cols), F32), vm((7, half, LANE), F32),
+            pltpu.SMEM((16,), jnp.int32), pltpu.SMEM((1, 4), F32), dma((2,)),
             dma((8,)), dma((8,)), dma((2, 8)), dma((2, 8)), dma((3,)), dma((3,)),
             dma((len(chunks), 16)), dma((len(chunks), 16)),
         ],
@@ -558,7 +624,7 @@
         ),
         in_specs=[vmem] * 5,
         out_specs=(hbm, hbm, hbm),
-        scratch_shapes=[vm((nrow, LANE), F32), vm((rows, cols), F32), dma((5,))],
+        scratch_shapes=[vm((nrow, LANE), F32), vm((rows, cols), F32), dma((8,))],
         compiler_params=pltpu.CompilerParams(vmem_limit_bytes=FINISH_VMEM),
         name="finish",
     )(*fields)

time: 50.9 us -> 45.2 us (0.89)
  Pallas kernels: 50.1 us -> 44.5 us
    pallas_call x1, Pallas kernels: 46 us -> 40.6 us  [shards(): merge(bed, land_mask, cell_class, weights, cond_params, wave_stress, hydr...]
where the time goes in v3:
time: 45.2 us; the launch traced here: 45.1 us
  Pallas kernels  44.5 us (98%)
  between operations  0.64 us (1%)
    pallas_call x1, Pallas kernels, shards(): merge(bed, land_mask, cell_class, weights, cond_params, wave_stress, hydr...  40.6 us
    pallas_call x1, Pallas kernels, shards(): pl.pallas_call(functools.partial(finish, rows, cols), out_shape=(jax.Shap...  3.83 us

profile of v3, /device:TPU:1, one launch (start us, length us, event | category | flops | bytes accessed | tf_op | source)
XLA Modules:
  0.0 45.1 jit_solution(9578247975311648112)
XLA Ops:
  0.6 40.6 %merge.1 = (f32[272,1152]{1,0:T(8,128)S(1)}, f32[272,1152]{1,0:T(8,128)S(1)}, f32[272,1152]{1,0:T(8,128)S(1)}, f32[272,1152]{1,0:T(8,128)S(1)}, f32[272,1024]{1,0:T(8,128)S(1)}) custom-call(f32[256,1024]{1,0:T(8,128)} %bed_h.1, s32[256,1024]{1,0:T(8,128)} %mask_h.1, s32[256,1024]{1,0:T(8,128)} %cls_h.1, s32[16]{0:T(128)} %wts_h.1, f32[1,4]{1,0:T(1,128)} %par_h.1, ...), custom_call_target="tpu_custom_call" | custom-call | tf_op jit(solution)/shard_map/merge/pallas_call | solution.py:615
  41.3 3.8 %finish.1 = (f32[256,1024]{1,0:T(8,128)}, f32[256,1024]{1,0:T(8,128)}, f32[1,3,256,1024]{3,2,1,0:T(8,128)}) custom-call(f32[272,1152]{1,0:T(8,128)S(1)} %get-tuple-element.8.E, f32[272,1152]{1,0:T(8,128)S(1)} %get-tuple-element.9.U, f32[272,1152]{1,0:T(8,128)S(1)} %get-tuple-element.10.V, f32[272,1152]{1,0:T(8,128)S(1)} %get-tuple-element.11.BED, ...), custom_call_target="tpu_custom_call" | custom-call | tf_op jit(solution)/shard_map/finish/pallas_call | solution.py:618

commit v4 on v3

--- a/solution.py
+++ b/solution.py
@@ -17,11 +17,12 @@
 NX = 4
 FAR_FIRST = ((1, 2), (1, 1), (1, 3), (0, 2), (1, 0), (0, 1), (0, 3))
 SKEW = 2
+FR_ROWS = 32
 PIN = True
 MERGE_VMEM = 56 << 20
 FINISH_VMEM = 16 << 20
-CHUNKS = (10, 7)
-SCHEDULE = ((10, (0,)), (13, (0,)), (17, (1, 1, 0, 1, 0, 1, 0, 1)))
+CHUNKS = (9, 8)
+SCHEDULE = ((9, (0,)), (12, (0,)), (17, (1, 1, 0, 1, 0, 1, 0, 1)))
 
 
 def east(y):
@@ -86,6 +87,7 @@
     wts,
     par,
     small_sem,
+    row_sem,
     in_sem,
     edge_sem,
     halo_send,
@@ -150,12 +152,18 @@
     ]
     for copy in edge_copies:
         copy.start()
+    ends = ((EDGE, 0), (EDGE + rows - 8, rows - 8))
+    row_copies = [
+        pltpu.make_async_copy(src.at[r : r + 8, :], dst.at[to : to + 8, 0:cols], row_sem.at[n, i])
+        for i, (src, dst) in enumerate(zip(sources, fields))
+        for n, (to, r) in enumerate(ends)
+    ]
+    for copy in row_copies:
+        copy.start()
     in_copies = [
-        pltpu.make_async_copy(src, dst.at[EDGE : EDGE + rows, 0:cols], in_sem.at[i])
+        pltpu.make_async_copy(src.at[8 : rows - 8, :], dst.at[EDGE + 8 : EDGE + rows - 8, 0:cols], in_sem.at[i])
         for i, (src, dst) in enumerate(zip(sources, fields))
     ]
-    for i in (5, 6, 0, 1, 2, 3, 4, 7):
-        in_copies[i].start()
 
     barrier = pltpu.get_barrier_semaphore()
     peers = (sibling, *partners, above, below, beside, diag_up, diag_down)
@@ -168,39 +176,11 @@
     for level in (E, E1, E2):
         level[nrow : nrow + 8, :] = jnp.zeros((8, width), F32)
     D[nrow : nrow + 8, :] = jnp.zeros((8, width), F32)
-    pl.semaphore_wait(barrier, len(peers))
-
-    def remote(src, dst, send, recv, peer):
-        copy = pltpu.make_async_remote_copy(
-            src_ref=src, dst_ref=dst, send_sem=send, recv_sem=recv, device_id=peer, device_id_type=MESH
-        )
-        copy.start()
-        return copy
-
-    halo_copies = []
-    for i, (src, dst) in enumerate(zip(sources, fields)):
-        halo_copies.append(
-            remote(
-                src.at[rows - HALO : rows, :],
-                dst.at[EDGE - HALO : EDGE, 0:cols],
-                halo_send.at[0, i],
-                halo_recv.at[0, i],
-                below,
-            )
-        )
-        halo_copies.append(
-            remote(
-                src.at[0:HALO, :],
-                dst.at[EDGE + rows : EDGE + rows + HALO, 0:cols],
-                halo_send.at[1, i],
-                halo_recv.at[1, i],
-                above,
-            )
-        )
-
     lanes = lax.broadcasted_iota(jnp.int32, (R, LANE), 1)
-    for copy in edge_copies:
+    for copy in edge_copies + row_copies:
         copy.wait()
+    for i in (5, 6, 7, 0, 1, 2, 3, 4):
+        in_copies[i].start()
 
     group = rows // GROUPS
 
@@ -217,6 +197,36 @@
         return carry
 
     lax.fori_loop(0, group // R, pack, 0)
+    pl.semaphore_wait(barrier, len(peers))
+
+    def remote(src, dst, send, recv, peer):
+        copy = pltpu.make_async_remote_copy(
+            src_ref=src, dst_ref=dst, send_sem=send, recv_sem=recv, device_id=peer, device_id_type=MESH
+        )
+        copy.start()
+        return copy
+
+    halo_copies = []
+    for i, dst in enumerate(fields):
+        halo_copies.append(
+            remote(
+                dst.at[EDGE + rows - HALO : EDGE + rows, 0:cols],
+                dst.at[EDGE - HALO : EDGE, 0:cols],
+                halo_send.at[0, i],
+                halo_recv.at[0, i],
+                below,
+            )
+        )
+        halo_copies.append(
+            remote(
+                dst.at[EDGE : EDGE + HALO, 0:cols],
+                dst.at[EDGE + rows : EDGE + rows + HALO, 0:cols],
+                halo_send.at[1, i],
+                halo_recv.at[1, i],
+                above,
+            )
+        )
+
     strip_copies = [
         remote(PS, RSTRIP.at[8 : 8 + group], strip_send.at[0], strip_recv.at[0], beside),
         remote(PS.at[group - 8 : group], RSTRIP.at[0:8], strip_send.at[1], strip_recv.at[1], diag_down),
@@ -405,17 +415,18 @@
         sweep((1, 2), goals[1] - done[1])
         sweep((2,), goals[2] - done[2])
 
-    def pack_column():
-        rolled = jnp.zeros((8, LANE), F32)
-        lane8 = lax.broadcasted_iota(jnp.int32, (8, LANE), 1)
-        sub8 = lax.broadcasted_iota(jnp.int32, (8, LANE), 0)
-
+    lane8 = lax.broadcasted_iota(jnp.int32, (8, LANE), 1)
+    sub8 = lax.broadcasted_iota(jnp.int32, (8, LANE), 0)
+
+    def pack_column(rolled, first, last):
         def take(k, acc):
             cells = T[pl.ds(pl.multiple_of(EDGE + 8 * k, 8), 8), cols:width]
             cells = pltpu.roll(cells, (k + tx) % LANE, 1)
             return jnp.where(lane8 == k, cells, acc)
 
-        rolled = lax.fori_loop(0, rows // 8, take, rolled, unroll=8)
+        return lax.fori_loop(first, last, take, rolled, unroll=8 if (last - first) % 8 == 0 else 5)
+
+    def place_column(rolled):
         last = T[nrow - 8 : nrow, 0:LANE]
         T[nrow - 8 : nrow, 0:LANE] = jnp.where(sub8 == 0, last, rolled)
         last = T[nrow - 8 : nrow, LANE : 2 * LANE]
@@ -502,12 +513,19 @@
             stages[at_stage[k]](k)
             at_stage[k] += 1
 
+    column, taken = jnp.zeros((8, LANE), F32), 0
     for stop, ready in schedule:
         run(stop)
+        if stop < nblk:
+            for k in ready:
+                progress(k)
+        packed = min(stop * R - EDGE, rows) // 8
+        column = pack_column(column, taken, packed)
+        taken = packed
         if stop == nblk:
-            pack_column()
-        for k in ready:
-            progress(k)
+            place_column(column)
+            for k in ready:
+                progress(k)
     while min(at_stage) < len(stages):
         for k in range(len(chunks)):
             progress(k)
@@ -543,31 +561,31 @@
     Z[nrow - EDGE : nrow, :] = jnp.zeros((EDGE, LANE), F32)
     lax.fori_loop(0, rows // 8, spread, 0, unroll=8)
 
-    place = lax.broadcasted_iota(jnp.int32, (R, width), 1)
-    rows24 = lax.broadcasted_iota(jnp.int32, (R + 8, width), 0)
+    place = lax.broadcasted_iota(jnp.int32, (FR_ROWS, width), 1)
+    rows24 = lax.broadcasted_iota(jnp.int32, (FR_ROWS + 8, width), 0)
     inside_c = (place < cols) & (tx * cols + place <= ntx * cols - 2) | (place == width - 1) & (tx > 0)
 
     def bed_update(i, carry):
-        r = pl.multiple_of(EDGE + i * R, 8)
-        at = pl.ds(r - 8, R + 16)
+        r = pl.multiple_of(EDGE + i * FR_ROWS, 8)
+        at = pl.ds(r - 8, FR_ROWS + 16)
         z = BED[at, :] + jnp.concatenate([M[at, :], Z[at, :]], axis=1)
-        mid = z[8 : 8 + R]
+        mid = z[8 : 8 + FR_ROWS]
         slope_c = jnp.where(inside_c, east(mid) - mid, 0.0)
         spill_c = 0.25 * (slope_c - jnp.clip(slope_c, -1.0, 1.0))
-        top = z[: R + 8]
-        at = rows24 + (ty * rows + i * R - 8)
-        below_z = pltpu.roll(z, R + 15, 0)[: R + 8]
+        top = z[: FR_ROWS + 8]
+        at = rows24 + (ty * rows + i * FR_ROWS - 8)
+        below_z = pltpu.roll(z, FR_ROWS + 15, 0)[: FR_ROWS + 8]
         slope_r = jnp.where((at >= 0) & (at <= nty * rows - 2), below_z - top, 0.0)
         spill_r = 0.25 * (slope_r - jnp.clip(slope_r, -1.0, 1.0))
         flow_r = (spill_r - pltpu.roll(spill_r, 1, 0))[8:]
         bed_new = mid + (spill_c - west(spill_c)) + flow_r
-        BN[pl.ds(pl.multiple_of(i * R, R), R), :] = bed_new[:, 0:cols]
+        BN[pl.ds(pl.multiple_of(i * FR_ROWS, R), FR_ROWS), :] = bed_new[:, 0:cols]
         return carry
 
-    parts = rows // R // 4
+    parts = rows // FR_ROWS // 4
     for part in range(4):
         lax.fori_loop(part * parts, (part + 1) * parts, bed_update, 0)
-        at = slice(part * parts * R, (part + 1) * parts * R)
+        at = slice(part * parts * FR_ROWS, (part + 1) * parts * FR_ROWS)
         copies.append(pltpu.make_async_copy(BN.at[at], bn_h.at[at], out_sem.at[4 + part]))
         copies[-1].start()
     for copy in copies:
@@ -604,7 +622,7 @@
             vm((rows // GROUPS, LANE), F32), vm((rows // GROUPS + 16, LANE), F32),
             vm((half, cols), F32), vm((half, cols), F32), vm((7, half, LANE), F32),
             pltpu.SMEM((16,), jnp.int32), pltpu.SMEM((1, 4), F32), dma((2,)),
-            dma((8,)), dma((8,)), dma((2, 8)), dma((2, 8)), dma((3,)), dma((3,)),
+            dma((2, 8)), dma((8,)), dma((8,)), dma((2, 8)), dma((2, 8)), dma((3,)), dma((3,)),
             dma((len(chunks), 16)), dma((len(chunks), 16)),
         ],
         compiler_params=pltpu.CompilerParams(

time: 45.2 us -> 43.8 us (0.969)
  Pallas kernels: 44.5 us -> 43 us
    pallas_call x1, Pallas kernels: 3.83 us -> 2.71 us  [shards(): pl.pallas_call(functools.partial(finish, rows, cols), out_shape=(jax.Shap...]
where the time goes in v4:
time: 43.8 us; the launch traced here: 43.6 us
  Pallas kernels  43 us (98%)
  between operations  0.64 us (1%)
    pallas_call x1, Pallas kernels, shards(): merge(bed, land_mask, cell_class, weights, cond_params, wave_stress, hydr...  40.3 us
    pallas_call x1, Pallas kernels, shards(): pl.pallas_call(functools.partial(finish, rows, cols), out_shape=(jax.Shap...  2.71 us

profile of v4, /device:TPU:1, one launch (start us, length us, event | category | flops | bytes accessed | tf_op | source)
XLA Modules:
  0.0 43.6 jit_solution(17200725879245732297)
XLA Ops:
  0.6 40.3 %merge.1 = (f32[272,1152]{1,0:T(8,128)S(1)}, f32[272,1152]{1,0:T(8,128)S(1)}, f32[272,1152]{1,0:T(8,128)S(1)}, f32[272,1152]{1,0:T(8,128)S(1)}, f32[272,1024]{1,0:T(8,128)S(1)}) custom-call(f32[256,1024]{1,0:T(8,128)} %bed_h.1, s32[256,1024]{1,0:T(8,128)} %mask_h.1, s32[256,1024]{1,0:T(8,128)} %cls_h.1, s32[16]{0:T(128)} %wts_h.1, f32[1,4]{1,0:T(1,128)} %par_h.1, ...), custom_call_target="tpu_custom_call" | custom-call | tf_op jit(solution)/shard_map/merge/pallas_call | solution.py:633
  40.9 2.7 %finish.1 = (f32[256,1024]{1,0:T(8,128)}, f32[256,1024]{1,0:T(8,128)}, f32[1,3,256,1024]{3,2,1,0:T(8,128)}) custom-call(f32[272,1152]{1,0:T(8,128)S(1)} %get-tuple-element.8.E, f32[272,1152]{1,0:T(8,128)S(1)} %get-tuple-element.9.U, f32[272,1152]{1,0:T(8,128)S(1)} %get-tuple-element.10.V, f32[272,1152]{1,0:T(8,128)S(1)} %get-tuple-element.11.BED, ...), custom_call_target="tpu_custom_call" | custom-call | tf_op jit(solution)/shard_map/finish/pallas_call | solution.py:636
